TPU v7x, 512 devices: a whole 4x8x8 slice. The times are simulated.
512 devices in a mesh: wave: 64 (over x, z, core), field: 8 (over y).
Axes of the slice: x: 4, y: 8, z: 8, core: 2. Of those that a mesh axis runs over, the one named last changes fastest.
Arguments:
- spectral: float32 [640, 1281, 2, 80], P('wave', None, None, 'field'), may hold values from -0.0078125 to 0.0078125
- legendre: bfloat16 [640, 1281, 128], P('wave'), may hold values from -6 to 6
- wave_pairs: int32 [640], P('wave'), may hold values from 0 to 639, each once
- npoints: int32 [256], replicated, may hold values from 20 to 5136, as said below
- lat_rows: int32 [256], P('wave'), may hold values from 0 to 255, as said below
Outputs:
- grid: bfloat16 [2, 80, 659968], P(None, None, ('wave', 'field'))
Inputs may be any that keep to these rules, and one draw needn't show every extreme that they name: Slot p holds wavenumbers wave_pairs[p] and 1279 - wave_pairs[p]; every wavenumber is held by exactly one slot. `npoints`: a latitude i rows from the nearer pole among 1280 has 4 i + 16 points; window latitudes 2 u and 2 u + 1 have 5156 points together. `lat_rows`: every window latitude appears once; the latitudes in slots 2 q and 2 q + 1 have 5156 points together.
All inputs are finite; a program needn't handle non-finite values.
Results may differ from a plain program's by a relative error of at most 0.0063.
Values may be sent and summed in bfloat16 or wider, within the bound.
No kernel may reach another device: no remote copies, remote signals or barrier semaphores. Data moves between devices by JAX's collectives and lax.ppermute only.
A program may use at most 192 MiB of HBM per device.

v0:
```python
import functools

import jax
import jax.numpy as jnp
import numpy as np
from jax import lax
from jax.experimental import pallas as pl
from jax.experimental.pallas import tpu as pltpu
from jax.sharding import PartitionSpec as P

ROW_PAIR = 5156
QUARTER = ROW_PAIR // 4
CHUNK = 256
PAIR_CHUNKS = 7
GROUPS = 5
TILES = 4
ROWS = 24
SIN = (6.283184905907144, -41.34158660945749, 81.59984497508991, -76.61321302879018, 41.33641025544816, -12.459753683550199)
COS = (0.999999988711474, -19.739204378854772, 64.93911099976975, -85.4500154366872, 60.16656814312298, -25.963448256110482, 6.5226306139218035)
f32, bf16, i32 = jnp.float32, jnp.bfloat16, jnp.int32


def legendre_kernel(truncation, waves, spec_ref, leg_ref, out_ref, coeffs):
    slot = pl.program_id(0)
    rows = truncation + 2
    fields = spec_ref.shape[1]

    @pl.when(slot == 0)
    def _():
        coeffs[...] = jnp.zeros_like(coeffs)

    for field in range(fields):
        coeffs[2 * field : 2 * field + 2, 0:rows] = spec_ref[0, field]
    split = truncation + 1 - waves[slot]
    row = lax.broadcasted_iota(i32, (1, rows), 1)
    low = row < split
    offset = jnp.where(low, row, row - split)
    sign = jnp.where(offset % 2 == 0, 1.0, -1.0).astype(f32)
    low = jnp.where(low, 1.0, 0.0).astype(f32)
    high = 1.0 - low
    values = coeffs[:, 0:rows]
    stacked = jnp.concatenate([values * mask for mask in (low, low * sign, high, high * sign)], axis=0)
    stacked = stacked.astype(bf16)
    main = rows - 1
    sums = jnp.dot(stacked[:, 0:main], leg_ref[0, 0:main, :], preferred_element_type=f32)
    last = stacked[:, main:rows].astype(f32) * leg_ref[0, main:rows, :].astype(f32)
    sums = sums + last
    for half in range(2):
        for side in range(2):
            at = (2 * half + side) * ROWS
            out_ref[half, :, 128 * side : 128 * side + 128] = sums[at : at + ROWS, :]


def legendre_sums(wave_pairs, spectral, legendre):
    slots, rows, northern = legendre.shape
    fields = spectral.shape[3]
    parts = jnp.transpose(spectral, (0, 3, 2, 1))
    return pl.pallas_call(
        functools.partial(legendre_kernel, rows - 2),
        out_shape=jax.ShapeDtypeStruct((2 * slots, ROWS, 2 * northern), f32),
        grid_spec=pltpu.PrefetchScalarGridSpec(
            num_scalar_prefetch=1,
            grid=(slots,),
            in_specs=[
                pl.BlockSpec((1, fields, 2, rows), lambda p, w: (p, 0, 0, 0)),
                pl.BlockSpec((1, rows, northern), lambda p, w: (p, 0, 0)),
            ],
            out_specs=pl.BlockSpec((2, ROWS, 2 * northern), lambda p, w: (p, 0, 0)),
            scratch_shapes=[pltpu.VMEM((ROWS, 1408), f32)],
        ),
    )(wave_pairs, parts, legendre)


def order_kernel(index_ref, sums_ref, out_ref, scratch):
    devices, lats = index_ref.shape[0], sums_ref.shape[2]
    lane = lax.broadcasted_iota(i32, (devices, lats), 1).astype(f32)
    onehot = jnp.concatenate(
        [jnp.where(index_ref[:, 10 + j : 11 + j] == lane, 1.0, 0.0) for j in range(4)], axis=0
    ).astype(bf16)
    for t in range(TILES):
        part = sums_ref[GROUPS * t : GROUPS * (t + 1)].reshape(GROUPS * ROWS, lats)
        part = jnp.concatenate([part, jnp.zeros((128 - GROUPS * ROWS, lats), f32)], axis=0).astype(bf16)
        picked = lax.dot_general(onehot, part, (((1,), (1,)), ((), ())), preferred_element_type=f32)
        for j in range(4):
            scratch[pl.ds(j * TILES + t, devices, 4 * TILES), :] = picked[devices * j : devices * (j + 1), :]
    out_ref[...] = scratch[...].reshape(out_ref.shape).astype(bf16)


def order_latitudes(index, sums):
    devices = index.shape[0]
    return pl.pallas_call(
        order_kernel,
        out_shape=jax.ShapeDtypeStruct((devices, 4 * TILES, 128), bf16),
        in_specs=[pl.BlockSpec(memory_space=pltpu.VMEM)] * 2,
        out_specs=pl.BlockSpec(memory_space=pltpu.VMEM),
        scratch_shapes=[pltpu.VMEM((devices * 4 * TILES, 128), f32)],
    )(index, sums)


def poly(coefficients, y):
    total = jnp.full_like(y, coefficients[-1])
    for c in coefficients[-2::-1]:
        total = total * y + c
    return total


def lat_scalars(lat_rows, npoints, l):
    points = npoints[lat_rows[l]]
    quarter = lax.shift_right_arithmetic(points, 2)
    chunks = lax.shift_right_arithmetic(quarter + (CHUNK - 1), 8)
    return points, quarter, chunks


BLOCK = 32


def table_kernel(truncation, lat_rows, npoints, index_ref, out_ref, waves):
    group = pl.program_id(0)
    devices = index_ref.shape[0]
    for g in range(GROUPS):

        @pl.when(group == g)
        def _():
            for t in range(TILES):
                ph = GROUPS * t + g
                column = index_ref[:, ph // 2 : ph // 2 + 1]
                if ph % 2:
                    column = truncation - column
                waves[devices * t : devices * (t + 1), :] = jnp.broadcast_to(column, (devices, 128))

    lane = lax.broadcasted_iota(i32, (BLOCK, 128), 1).astype(f32)
    first = [0, None, PAIR_CHUNKS, None]
    points, counts = [], []
    for l in range(4):
        n, _, count = lat_scalars(lat_rows, npoints, l)
        points.append(n)
        counts.append(count)
    first[1] = counts[0]
    first[3] = PAIR_CHUNKS + counts[2]

    def rows_block(r, carry):
        at = pl.multiple_of(r * BLOCK, BLOCK)
        k = waves[pl.ds(at, BLOCK), :]
        product = k * lane
        weight = jnp.where(k == 0.0, 1.0, 2.0)
        for l in range(4):
            n = jnp.full((BLOCK, 128), points[l], i32).astype(f32)
            inverse = 1.0 / n
            turns = jnp.floor(product * inverse + 0.5)
            f = (product - turns * n) * inverse
            y = f * f
            real = poly(COS, y)
            imag = poly(SIN, y) * f
            c64 = jnp.broadcast_to(real[:, 64:65], (BLOCK, 128))
            s64 = jnp.broadcast_to(imag[:, 64:65], (BLOCK, 128))
            c128 = 2.0 * c64 * c64 - 1.0
            s128 = 2.0 * c64 * s64
            scale = jnp.where(2.0 * k < n, weight, 0.0)
            real = real * scale
            imag = imag * (-scale)
            step = 2.0 * c128
            real_before = real * c128 - imag * s128
            imag_before = imag * c128 + real * s128

            def chunk(c, state):
                ra, ia, rb, ib = state
                rc = step * rb - ra
                ic = step * ib - ia
                to = first[l] + c
                out_ref[to, 0, pl.ds(at, BLOCK), 0:128] = rb.astype(bf16)
                out_ref[to, 0, pl.ds(at, BLOCK), 128:256] = rc.astype(bf16)
                out_ref[to, 1, pl.ds(at, BLOCK), 0:128] = ib.astype(bf16)
                out_ref[to, 1, pl.ds(at, BLOCK), 128:256] = ic.astype(bf16)
                return rc, ic, step * rc - rb, step * ic - ib

            lax.fori_loop(0, counts[l], chunk, (real_before, imag_before, real, imag))
        return carry

    lax.fori_loop(0, TILES * devices // BLOCK, rows_block, 0)


def fourier_tables(lat_rows, npoints, index, truncation):
    devices = index.shape[0]
    rows = TILES * devices
    return pl.pallas_call(
        functools.partial(table_kernel, float(truncation)),
        out_shape=jax.ShapeDtypeStruct((2 * PAIR_CHUNKS, 2, GROUPS * rows, CHUNK), bf16),
        grid_spec=pltpu.PrefetchScalarGridSpec(
            num_scalar_prefetch=2,
            grid=(GROUPS,),
            in_specs=[pl.BlockSpec((devices, 128), lambda g, a, b: (0, 0))],
            out_specs=pl.BlockSpec((2 * PAIR_CHUNKS, 2, rows, CHUNK), lambda g, a, b: (0, 0, g, 0)),
            scratch_shapes=[pltpu.VMEM((rows, 128), f32)],
        ),
        compiler_params=pltpu.CompilerParams(vmem_limit_bytes=32 << 20),
    )(lat_rows, npoints, index)


def synthesis_kernel(truncation, lat_rows, npoints, got_ref, wave_ref, select_ref, table_ref, out_ref, got, left, right, line):
    pair, step = pl.program_id(0), pl.program_id(1)
    devices = got_ref.shape[0]
    rows = TILES * devices

    @pl.when((pair == 0) & (step == 0))
    def _():
        got[...] = got_ref[...].reshape(devices * 4 * TILES, 128).astype(f32)
        line[...] = jnp.zeros_like(line)
        for l in range(4):
            stacked = jnp.concatenate(
                [got[pl.ds(l * TILES + t, devices, 4 * TILES), :] for t in range(TILES)], axis=0
            ).astype(bf16)
            both = lax.dot_general(select_ref[...], stacked, (((1,), (1,)), ((), ())), preferred_element_type=f32)
            for g in range(GROUPS):
                k = wave_ref[:, g * rows : (g + 1) * rows]
                row = lax.broadcasted_iota(i32, (ROWS, rows), 0)
                scale = jnp.where(row < 10, 1.0, jnp.broadcast_to(k / truncation, (ROWS, rows)))
                at = 2 * ROWS * g
                real = (both[at : at + ROWS] * scale).astype(bf16).astype(f32)
                imag = (both[at + ROWS : at + 2 * ROWS] * scale).astype(bf16).astype(f32)
                for a in range(4):
                    turn = a * k
                    turn = turn - 4.0 * jnp.floor(turn * 0.25)
                    cr = jnp.where(turn == 0.0, 1.0, jnp.where(turn == 2.0, -1.0, 0.0))
                    ci = jnp.where(turn == 1.0, 1.0, jnp.where(turn == 3.0, -1.0, 0.0))
                    left[l, a * ROWS : (a + 1) * ROWS, g * rows : (g + 1) * rows] = (real * cr - imag * ci).astype(bf16)
                    right[l, a * ROWS : (a + 1) * ROWS, g * rows : (g + 1) * rows] = (imag * cr + real * ci).astype(bf16)

    n_a, m_a, count_a = lat_scalars(lat_rows, npoints, 2 * pair)
    _, m_b, count_b = lat_scalars(lat_rows, npoints, 2 * pair + 1)
    second = step >= count_a
    l = 2 * pair + jnp.where(second, 1, 0)
    c = jnp.where(second, step - count_a, step)
    m = jnp.where(second, m_b, m_a)
    base = jnp.where(second, n_a, 0) + CHUNK * c
    length = m - CHUNK * c

    @pl.when(step < count_a + count_b)
    def _():
        values = jnp.dot(left[l], table_ref[0, 0], preferred_element_type=f32)
        values = values + jnp.dot(right[l], table_ref[0, 1], preferred_element_type=f32)
        lane = lax.broadcasted_iota(i32, (ROWS, 128), 1)
        for a in range(4):
            off = base + a * m
            tile = lax.shift_right_arithmetic(off, 7)
            shift = off & 127
            v0 = pltpu.roll(values[a * ROWS : (a + 1) * ROWS, 0:128], shift, 1)
            v1 = pltpu.roll(values[a * ROWS : (a + 1) * ROWS, 128:256], shift, 1)
            after = lane >= shift
            at = lane - shift
            line[tile] = jnp.where(after & (at < length), v0, line[tile])
            line[tile + 1] = jnp.where(at + 128 < length, jnp.where(after, v1, v0), line[tile + 1])
            line[tile + 2] = jnp.where(jnp.logical_not(after) & (at + 256 < length), v1, line[tile + 2])

    @pl.when(step == PAIR_CHUNKS - 1)
    def _():
        lane = lax.broadcasted_iota(i32, (ROWS, 128), 1)
        for q in range(4):
            shift = (QUARTER * q) % 128
            for i in range(QUARTER // 128 + 1):
                tile = QUARTER * q // 128 + i
                v = line[tile]
                if shift:
                    v = jnp.where(
                        lane < 128 - shift,
                        pltpu.roll(v, 128 - shift, 1),
                        pltpu.roll(line[tile + 1], 128 - shift, 1),
                    )
                width = min(128, QUARTER - 128 * i)
                out_ref[q, :, 128 * i : 128 * i + width] = v[0 : out_ref.shape[1], 0:width].astype(bf16)


def select_rows():
    table = np.zeros((GROUPS, 2 * ROWS, 128), np.float32)
    for g in range(GROUPS):
        for f in range(10):
            real, imag = g * ROWS + 2 * f, g * ROWS + 2 * f + 1
            table[g, f, real] = 1.0
            table[g, 10 + f, imag] = -1.0
            table[g, ROWS + f, imag] = 1.0
            table[g, ROWS + 10 + f, real] = 1.0
    return table.reshape(GROUPS * 2 * ROWS, 128).astype(jnp.bfloat16)


def synthesis(lat_rows, npoints, received, wave_line, tables, truncation):
    devices = received.shape[0]
    depth = GROUPS * TILES * devices

    def table_at(pair, step, lats, points):
        total = lat_scalars(lats, points, 2 * pair)[2] + lat_scalars(lats, points, 2 * pair + 1)[2]
        return (pair * PAIR_CHUNKS + jnp.minimum(step, total - 1), 0, 0, 0)

    return pl.pallas_call(
        functools.partial(synthesis_kernel, float(truncation)),
        out_shape=jax.ShapeDtypeStruct((8, 20, QUARTER), bf16),
        grid_spec=pltpu.PrefetchScalarGridSpec(
            num_scalar_prefetch=2,
            grid=(2, PAIR_CHUNKS),
            in_specs=[
                pl.BlockSpec((devices, 4 * TILES, 128), lambda p, s, a, b: (0, 0, 0)),
                pl.BlockSpec((1, depth), lambda p, s, a, b: (0, 0)),
                pl.BlockSpec((GROUPS * 2 * ROWS, 128), lambda p, s, a, b: (0, 0)),
                pl.BlockSpec((1, 2, depth, CHUNK), table_at),
            ],
            out_specs=pl.BlockSpec((4, 20, QUARTER), lambda p, s, a, b: (p, 0, 0)),
            scratch_shapes=[
                pltpu.VMEM((devices * 4 * TILES, 128), f32),
                pltpu.VMEM((4, 4 * ROWS, depth), bf16),
                pltpu.VMEM((4, 4 * ROWS, depth), bf16),
                pltpu.VMEM((44, ROWS, 128), f32),
            ],
        ),
        compiler_params=pltpu.CompilerParams(vmem_limit_bytes=32 << 20),
    )(lat_rows, npoints, received, wave_line, select_rows(), tables)


def wave_line_of(index, truncation):
    low = jnp.transpose(index[:, 0:10])
    both = jnp.stack([low, truncation - low], axis=1)
    both = both.reshape(TILES, GROUPS, index.shape[0])
    return jnp.transpose(both, (1, 0, 2)).reshape(1, -1)


def on_device(spectral, legendre, wave_pairs, npoints, lat_rows):
    truncation = legendre.shape[1] - 2
    devices = lax.axis_size("wave")
    mine = jnp.concatenate([wave_pairs, lat_rows]).astype(f32)
    mine = jnp.pad(mine, (0, 128 - mine.shape[0]))
    index = lax.all_to_all(jnp.broadcast_to(mine[None, None, :], (devices, 1, 128)), "wave", 0, 0, tiled=True)
    index = index.reshape(devices, 128)
    sums = legendre_sums(wave_pairs, spectral, legendre)
    ordered = order_latitudes(index, sums)
    received = lax.all_to_all(ordered, "wave", 0, 0, tiled=True)
    tables = fourier_tables(lat_rows, npoints, index, truncation)
    wave_line = wave_line_of(index, float(truncation))
    blocks = synthesis(lat_rows, npoints, received, wave_line, tables, truncation)
    blocks = lax.all_to_all(blocks, "field", 0, 0, tiled=True)
    blocks = blocks.reshape(8, 2, 10, QUARTER)
    return jnp.transpose(blocks, (1, 0, 2, 3)).reshape(2, 80, QUARTER)


def solution(mesh):
    placed = (P("wave", None, None, "field"), P("wave", None, None), P("wave"), P(), P("wave"))
    return jax.shard_map(
        on_device,
        mesh=mesh,
        in_specs=placed,
        out_specs=P(None, None, ("wave", "field")),
        check_vma=False,
    )
```

profile of v0, /device:TPU:6, one launch (start us, length us, event | category | flops | bytes accessed | tf_op | source)
XLA Modules:
  0.0 108.9 jit_solution(8764613516543869704)
XLA Ops:
  0.0 0.7 add_convert_fusion
  0.8 0.6 broadcast_in_dim.2
  1.4 0.0 copy-start.5
  1.4 0.0 copy-start.6
  1.4 14.1 %all-to-all-start = ((f32[64,1,128]{2,1,0:T(1,128)}), f32[64,1,128]{2,1,0:T(1,128)S(1)}, u32[]{:S(2)}, u32[]{:S(2)}) async-start(f32[64,1,128]{2,1,0:T(1,128)} %broadcast_in_dim.2), calls=%async_computation | async-start | bytes 65536 | tf_op jit(solution)/shard_map/all_to_all | solution.py:328
  15.6 8.5 %shard_map.64.sums_ref = f32[20,24,256]{2,1,0:T(8,128)} custom-call(s32[10]{0:T(128)} %waves.1, f32[10,10,2,1281]{3,2,1,0:T(2,128)} %bitcast.22, bf16[10,1281,128]{2,1,0:T(8,128)(2,1)} %leg_ref.1), custom_call_target="tpu_custom_call" | custom-call | tf_op jit(solution)/shard_map/pallas_call | solution.py:58
  24.1 0.0 all-to-all-done
  24.1 0.0 copy-start.2
  24.1 0.6 copy-done.2
  24.7 2.2 %shard_map.65 = bf16[64,16,128]{2,1,0:T(8,128)(2,1)} custom-call(f32[64,128]{1,0:T(8,128)} %bitcast.16, f32[20,24,256]{2,1,0:T(8,128)} %shard_map.64.sums_ref), custom_call_target="tpu_custom_call" | custom-call | tf_op jit(solution)/shard_map/pallas_call | solution.py:91
  26.8 10.3 %all-to-all-start.1 = ((bf16[64,16,128]{2,1,0:T(8,128)(2,1)}), bf16[64,16,128]{2,1,0:T(8,128)(2,1)S(1)}, u32[]{:S(2)}, u32[]{:S(2)}) async-start(bf16[64,16,128]{2,1,0:T(8,128)(2,1)} %shard_map.65), calls=%async_computation.1 | async-start | bytes 524288 | tf_op jit(solution)/shard_map/all_to_all | solution.py:332
  37.2 0.8 slice_bitcast_fusion
  37.9 0.1 copy.13
  38.0 0.8 fusion
  38.8 0.1 copy.14
  38.9 0.1 reshape.20.wave_ref
  39.0 0.0 copy-done.5
  39.0 0.0 copy-done.6
  39.0 0.0 copy-start.3
  39.0 0.7 copy-done.3
  39.8 0.0 copy-start.4
  39.8 22.9 %shard_map.66.table_ref = bf16[14,2,1280,256]{3,2,1,0:T(8,128)(2,1)S(1)} custom-call(s32[4]{0:T(128)S(1)} %copy-done.6, s32[256]{0:T(256)S(1)} %copy-done.5, f32[64,128]{1,0:T(8,128)S(1)} %bitcast.19), custom_call_target="tpu_custom_call" | custom-call | tf_op jit(solution)/shard_map/pallas_call | solution.py:185
  62.6 0.0 copy-start
  62.6 6.3 %copy-done = bf16[14,2,1280,256]{3,2,1,0:T(8,128)(2,1)} copy-done((bf16[14,2,1280,256]{3,2,1,0:T(8,128)(2,1)}, bf16[14,2,1280,256]{3,2,1,0:T(8,128)(2,1)S(1)}, u32[]{:S(2)}) %copy-start) | copy-done | bytes 18350104
  68.9 0.0 all-to-all-done.1.got_ref
  68.9 0.0 copy-done.4
  68.9 0.0 copy-start.1
  68.9 6.2 %copy-done.1 = bf16[14,2,1280,256]{3,2,1,0:T(8,128)(2,1)S(1)} copy-done((bf16[14,2,1280,256]{3,2,1,0:T(8,128)(2,1)S(1)}, bf16[14,2,1280,256]{3,2,1,0:T(8,128)(2,1)}, u32[]{:S(2)}) %copy-start.1) | copy-done | bytes 18350104
  75.1 7.5 %shard_map.67 = bf16[8,20,1289]{2,1,0:T(8,128)(2,1)S(1)} custom-call(s32[4]{0:T(128)S(1)} %copy-done.6, s32[256]{0:T(256)S(1)} %copy-done.5, bf16[64,16,128]{2,1,0:T(8,128)(2,1)S(1)} %all-to-all-done.1.got_ref, f32[1,1280]{1,0:T(1,128)S(1)} %reshape.20.wave_ref, bf16[240,128]{1,0:T(8,128)(2,1)S(1)} %copy-done.4, bf16[14,2,1280,256]{3,2,1,0:T(8,128)(2,1)S(1)} %copy-done.1), custom_call_target="tpu_custom_call" | custom-call | tf_op jit(solution)/shard_map/pallas_call | solution.py:292
  82.6 25.1 %all_to_all.15 = bf16[8,20,1289]{2,1,0:T(8,128)(2,1)S(1)} all-to-all(bf16[8,20,1289]{2,1,0:T(8,128)(2,1)S(1)} %shard_map.67), channel_id=1, replica_groups=mesh['wave'=64,'field'=8] {'field'}, dimensions={0} | all-to-all | bytes 824960 | tf_op jit(solution)/shard_map/all_to_all | solution.py:336
  107.7 0.3 copy.17
  108.1 0.8 copy.18
  (5 shorter events, 0.1 us)
Async XLA Ops:
  1.4 37.6 %copy-start.5 = (s32[256]{0:T(256)S(1)}, s32[256]{0:T(256)}, u32[]{:S(2)}) copy-start(s32[256]{0:T(256)} %npoints.3) | copy-start | bytes 3076
  1.4 37.6 %copy-start.6 = (s32[4]{0:T(128)S(1)}, s32[4]{0:T(128)}, u32[]{:S(2)}) copy-start(s32[4]{0:T(128)} %lat_rows.3) | copy-start | bytes 52
  1.4 22.7 %all-to-all-start = ((f32[64,1,128]{2,1,0:T(1,128)}), f32[64,1,128]{2,1,0:T(1,128)S(1)}, u32[]{:S(2)}, u32[]{:S(2)}) async-start(f32[64,1,128]{2,1,0:T(1,128)} %broadcast_in_dim.2), calls=%async_computation | async-start | bytes 65536 | tf_op jit(solution)/shard_map/all_to_all | solution.py:328
  24.1 0.6 copy-start.2
  26.8 42.1 %all-to-all-start.1 = ((bf16[64,16,128]{2,1,0:T(8,128)(2,1)}), bf16[64,16,128]{2,1,0:T(8,128)(2,1)S(1)}, u32[]{:S(2)}, u32[]{:S(2)}) async-start(bf16[64,16,128]{2,1,0:T(8,128)(2,1)} %shard_map.65), calls=%async_computation.1 | async-start | bytes 524288 | tf_op jit(solution)/shard_map/all_to_all | solution.py:332
  39.0 0.8 copy-start.3
  39.8 29.2 %copy-start.4 = (bf16[240,128]{1,0:T(8,128)(2,1)S(1)}, bf16[240,128]{1,0:T(8,128)(2,1)}, u32[]{:S(2)}) copy-start(bf16[240,128]{1,0:T(8,128)(2,1)} %constant.7.clone.select_ref) | copy-start | bytes 184324
  62.6 6.3 %copy-start = (bf16[14,2,1280,256]{3,2,1,0:T(8,128)(2,1)}, bf16[14,2,1280,256]{3,2,1,0:T(8,128)(2,1)S(1)}, u32[]{:S(2)}) copy-start(bf16[14,2,1280,256]{3,2,1,0:T(8,128)(2,1)S(1)} %shard_map.66.table_ref) | copy-start | bytes 55050244
  68.9 6.2 %copy-start.1 = (bf16[14,2,1280,256]{3,2,1,0:T(8,128)(2,1)S(1)}, bf16[14,2,1280,256]{3,2,1,0:T(8,128)(2,1)}, u32[]{:S(2)}) copy-start(bf16[14,2,1280,256]{3,2,1,0:T(8,128)(2,1)} %copy-done) | copy-start | bytes 55050244
where the time goes:
time: 111 us; the launch traced here: 109 us
  Pallas kernels  41 us (37%)
  blocking collectives  25.1 us (23%)
  starting transfers between devices  24.5 us (22%)
  local copies, waits for them, and re-layouts  16.7 us (15%)
  other arithmetic  1.54 us (1%)
    all_to_all x1, blocking collectives, on_device(): blocks = lax.all_to_all(blocks, 'field', 0, 0, tiled=True)  25.1 us
    pallas_call x1, Pallas kernels, fourier_tables(): pl.pallas_call(functools.partial(table_kernel, float(truncation)), out_sh...  22.9 us
    all_to_all x1, starting transfers between devices, on_device(): lax.all_to_all(jnp.broadcast_to(mine[None, None, :], (devices, 1, 128)),...  14.1 us
    unnamed x14, local copies, waits for them, and re-layouts  13.9 us
    all_to_all x1, starting transfers between devices, on_device(): received = lax.all_to_all(ordered, 'wave', 0, 0, tiled=True)  10.3 us
    pallas_call x1, Pallas kernels, legendre_sums(): pl.pallas_call(functools.partial(legendre_kernel, rows - 2), out_shape=ja...  8.5 us
    pallas_call x1, Pallas kernels, synthesis(): pl.pallas_call(functools.partial(synthesis_kernel, float(truncation)), ou...  7.48 us
  transfers between devices with their start and end apart: 2, of which 0 were waited for; matrix products, arithmetic and copies ran while one was open for 2% of the time, Pallas kernels for 29%

commit v1 on v0

--- a/solution.py
+++ b/solution.py
@@ -11,7 +11,6 @@
 ROW_PAIR = 5156
 QUARTER = ROW_PAIR // 4
 CHUNK = 256
-PAIR_CHUNKS = 7
 GROUPS = 5
 TILES = 4
 ROWS = 24
@@ -104,107 +103,95 @@
     return total
 
 
-def lat_scalars(lat_rows, npoints, l):
-    points = npoints[lat_rows[l]]
-    quarter = lax.shift_right_arithmetic(points, 2)
-    chunks = lax.shift_right_arithmetic(quarter + (CHUNK - 1), 8)
-    return points, quarter, chunks
-
-
-BLOCK = 32
+def sincos(product, n, inverse):
+    turns = jnp.floor(product * inverse + 0.5)
+    f = (product - turns * n) * inverse
+    y = f * f
+    return poly(COS, y), poly(SIN, y) * f
+
+
+BLOCK = 64
 
 
 def table_kernel(truncation, lat_rows, npoints, index_ref, out_ref, waves):
-    group = pl.program_id(0)
+    l = pl.program_id(0)
     devices = index_ref.shape[0]
-    for g in range(GROUPS):
-
-        @pl.when(group == g)
-        def _():
+    depth = GROUPS * TILES * devices
+
+    @pl.when(l == 0)
+    def _():
+        for g in range(GROUPS):
             for t in range(TILES):
                 ph = GROUPS * t + g
                 column = index_ref[:, ph // 2 : ph // 2 + 1]
                 if ph % 2:
                     column = truncation - column
-                waves[devices * t : devices * (t + 1), :] = jnp.broadcast_to(column, (devices, 128))
+                at = devices * (TILES * g + t)
+                waves[at : at + devices, :] = jnp.broadcast_to(column, (devices, 128))
 
     lane = lax.broadcasted_iota(i32, (BLOCK, 128), 1).astype(f32)
-    first = [0, None, PAIR_CHUNKS, None]
-    points, counts = [], []
-    for l in range(4):
-        n, _, count = lat_scalars(lat_rows, npoints, l)
-        points.append(n)
-        counts.append(count)
-    first[1] = counts[0]
-    first[3] = PAIR_CHUNKS + counts[2]
+    n = jnp.full((8, 128), npoints[lat_rows[l]], i32).astype(f32)
+    inverse = 1.0 / n
+    n, inverse = n[0:1], inverse[0:1]
 
     def rows_block(r, carry):
         at = pl.multiple_of(r * BLOCK, BLOCK)
         k = waves[pl.ds(at, BLOCK), :]
-        product = k * lane
-        weight = jnp.where(k == 0.0, 1.0, 2.0)
-        for l in range(4):
-            n = jnp.full((BLOCK, 128), points[l], i32).astype(f32)
-            inverse = 1.0 / n
-            turns = jnp.floor(product * inverse + 0.5)
-            f = (product - turns * n) * inverse
-            y = f * f
-            real = poly(COS, y)
-            imag = poly(SIN, y) * f
-            c64 = jnp.broadcast_to(real[:, 64:65], (BLOCK, 128))
-            s64 = jnp.broadcast_to(imag[:, 64:65], (BLOCK, 128))
-            c128 = 2.0 * c64 * c64 - 1.0
-            s128 = 2.0 * c64 * s64
-            scale = jnp.where(2.0 * k < n, weight, 0.0)
-            real = real * scale
-            imag = imag * (-scale)
-            step = 2.0 * c128
-            real_before = real * c128 - imag * s128
-            imag_before = imag * c128 + real * s128
-
-            def chunk(c, state):
-                ra, ia, rb, ib = state
-                rc = step * rb - ra
-                ic = step * ib - ia
-                to = first[l] + c
-                out_ref[to, 0, pl.ds(at, BLOCK), 0:128] = rb.astype(bf16)
-                out_ref[to, 0, pl.ds(at, BLOCK), 128:256] = rc.astype(bf16)
-                out_ref[to, 1, pl.ds(at, BLOCK), 0:128] = ib.astype(bf16)
-                out_ref[to, 1, pl.ds(at, BLOCK), 128:256] = ic.astype(bf16)
-                return rc, ic, step * rc - rb, step * ic - ib
-
-            lax.fori_loop(0, counts[l], chunk, (real_before, imag_before, real, imag))
+        real, imag = sincos(k * lane, n, inverse)
+        c64 = jnp.broadcast_to(real[:, 64:65], (BLOCK, 128))
+        s64 = jnp.broadcast_to(imag[:, 64:65], (BLOCK, 128))
+        c128 = 2.0 * c64 * c64 - 1.0
+        s128 = 2.0 * c64 * s64
+        scale = jnp.where(2.0 * k < n, jnp.where(k == 0.0, 1.0, 2.0), 0.0)
+        real = real * scale
+        imag = imag * scale
+        out_ref[0, pl.ds(at, BLOCK), 0:128] = real.astype(bf16)
+        out_ref[0, pl.ds(at, BLOCK), 128:256] = (real * c128 - imag * s128).astype(bf16)
+        out_ref[0, pl.ds(depth + at, BLOCK), 0:128] = (-imag).astype(bf16)
+        out_ref[0, pl.ds(depth + at, BLOCK), 128:256] = (-imag * c128 - real * s128).astype(bf16)
         return carry
 
-    lax.fori_loop(0, TILES * devices // BLOCK, rows_block, 0)
+    lax.fori_loop(0, depth // BLOCK, rows_block, 0)
 
 
 def fourier_tables(lat_rows, npoints, index, truncation):
     devices = index.shape[0]
-    rows = TILES * devices
+    depth = GROUPS * TILES * devices
     return pl.pallas_call(
         functools.partial(table_kernel, float(truncation)),
-        out_shape=jax.ShapeDtypeStruct((2 * PAIR_CHUNKS, 2, GROUPS * rows, CHUNK), bf16),
+        out_shape=jax.ShapeDtypeStruct((4, 2 * depth, CHUNK), bf16),
         grid_spec=pltpu.PrefetchScalarGridSpec(
             num_scalar_prefetch=2,
-            grid=(GROUPS,),
-            in_specs=[pl.BlockSpec((devices, 128), lambda g, a, b: (0, 0))],
-            out_specs=pl.BlockSpec((2 * PAIR_CHUNKS, 2, rows, CHUNK), lambda g, a, b: (0, 0, g, 0)),
-            scratch_shapes=[pltpu.VMEM((rows, 128), f32)],
+            grid=(4,),
+            in_specs=[pl.BlockSpec((devices, 128), lambda l, a, b: (0, 0))],
+            out_specs=pl.BlockSpec((1, 2 * depth, CHUNK), lambda l, a, b: (l, 0, 0)),
+            scratch_shapes=[pltpu.VMEM((depth, 128), f32)],
         ),
-        compiler_params=pltpu.CompilerParams(vmem_limit_bytes=32 << 20),
     )(lat_rows, npoints, index)
 
 
-def synthesis_kernel(truncation, lat_rows, npoints, got_ref, wave_ref, select_ref, table_ref, out_ref, got, left, right, line):
+BATCH = 8
+STEPS = 4
+LAST = ROW_PAIR // CHUNK
+
+
+def pair_batches(lat_rows, npoints, pair):
+    n_a = npoints[lat_rows[2 * pair]]
+    start_b = lax.shift_right_arithmetic(n_a, 8)
+    batches_a = lax.shift_right_arithmetic(lax.shift_right_arithmetic(n_a - 1, 8) + BATCH, 3)
+    batches_b = lax.shift_right_arithmetic(LAST - start_b + BATCH, 3)
+    return n_a, start_b, batches_a, batches_a + batches_b
+
+
+def synthesis_kernel(truncation, lat_rows, npoints, got_ref, wave_ref, select_ref, table_ref, out_ref, got, parts, left, line):
     pair, step = pl.program_id(0), pl.program_id(1)
     devices = got_ref.shape[0]
     rows = TILES * devices
+    depth = GROUPS * rows
 
     @pl.when((pair == 0) & (step == 0))
     def _():
         got[...] = got_ref[...].reshape(devices * 4 * TILES, 128).astype(f32)
-        line[...] = jnp.zeros_like(line)
         for l in range(4):
             stacked = jnp.concatenate(
                 [got[pl.ds(l * TILES + t, devices, 4 * TILES), :] for t in range(TILES)], axis=0
@@ -215,43 +202,47 @@
                 row = lax.broadcasted_iota(i32, (ROWS, rows), 0)
                 scale = jnp.where(row < 10, 1.0, jnp.broadcast_to(k / truncation, (ROWS, rows)))
                 at = 2 * ROWS * g
-                real = (both[at : at + ROWS] * scale).astype(bf16).astype(f32)
-                imag = (both[at + ROWS : at + 2 * ROWS] * scale).astype(bf16).astype(f32)
-                for a in range(4):
-                    turn = a * k
-                    turn = turn - 4.0 * jnp.floor(turn * 0.25)
-                    cr = jnp.where(turn == 0.0, 1.0, jnp.where(turn == 2.0, -1.0, 0.0))
-                    ci = jnp.where(turn == 1.0, 1.0, jnp.where(turn == 3.0, -1.0, 0.0))
-                    left[l, a * ROWS : (a + 1) * ROWS, g * rows : (g + 1) * rows] = (real * cr - imag * ci).astype(bf16)
-                    right[l, a * ROWS : (a + 1) * ROWS, g * rows : (g + 1) * rows] = (imag * cr + real * ci).astype(bf16)
-
-    n_a, m_a, count_a = lat_scalars(lat_rows, npoints, 2 * pair)
-    _, m_b, count_b = lat_scalars(lat_rows, npoints, 2 * pair + 1)
-    second = step >= count_a
+                for c in range(2):
+                    part = both[at + c * ROWS : at + (c + 1) * ROWS] * scale
+                    parts[l, c, :, g * rows : (g + 1) * rows] = part.astype(bf16).astype(f32)
+
+    n_a, start_b, batches_a, batches = pair_batches(lat_rows, npoints, pair)
+    second = step >= batches_a
     l = 2 * pair + jnp.where(second, 1, 0)
-    c = jnp.where(second, step - count_a, step)
-    m = jnp.where(second, m_b, m_a)
-    base = jnp.where(second, n_a, 0) + CHUNK * c
-    length = m - CHUNK * c
-
-    @pl.when(step < count_a + count_b)
-    def _():
-        values = jnp.dot(left[l], table_ref[0, 0], preferred_element_type=f32)
-        values = values + jnp.dot(right[l], table_ref[0, 1], preferred_element_type=f32)
+    first = jnp.where(second, start_b + BATCH * (step - batches_a), BATCH * step)
+    origin = jnp.where(second, n_a, 0)
+
+    @pl.when(step < batches)
+    def _():
+        n = jnp.full((8, 128), npoints[lat_rows[l]], i32).astype(f32)
+        inverse = (1.0 / n)[0:1, 0:1]
+        n = n[0:1, 0:1]
+        chunk = lax.broadcasted_iota(i32, (BATCH, rows), 0)
+        t0 = ((first + chunk) * CHUNK - origin).astype(f32)
+        for g in range(GROUPS):
+            at = slice(g * rows, (g + 1) * rows)
+            k = wave_ref[:, at]
+            cosine, sine = sincos(t0 * k, n, inverse)
+            real, imag = parts[l, 0, :, at], parts[l, 1, :, at]
+            for j in range(0, BATCH, 2):
+                turned = [
+                    (real * cosine[i : i + 1] - imag * sine[i : i + 1], imag * cosine[i : i + 1] + real * sine[i : i + 1])
+                    for i in (j, j + 1)
+                ]
+                to = slice(j * ROWS, (j + 2) * ROWS)
+                left[to, at] = jnp.concatenate([turned[0][0], turned[1][0]], axis=0).astype(bf16)
+                at_imag = slice(depth + g * rows, depth + (g + 1) * rows)
+                left[to, at_imag] = jnp.concatenate([turned[0][1], turned[1][1]], axis=0).astype(bf16)
+        values = jnp.dot(left[...], table_ref[0], preferred_element_type=f32)
         lane = lax.broadcasted_iota(i32, (ROWS, 128), 1)
-        for a in range(4):
-            off = base + a * m
-            tile = lax.shift_right_arithmetic(off, 7)
-            shift = off & 127
-            v0 = pltpu.roll(values[a * ROWS : (a + 1) * ROWS, 0:128], shift, 1)
-            v1 = pltpu.roll(values[a * ROWS : (a + 1) * ROWS, 128:256], shift, 1)
-            after = lane >= shift
-            at = lane - shift
-            line[tile] = jnp.where(after & (at < length), v0, line[tile])
-            line[tile + 1] = jnp.where(at + 128 < length, jnp.where(after, v1, v0), line[tile + 1])
-            line[tile + 2] = jnp.where(jnp.logical_not(after) & (at + 256 < length), v1, line[tile + 2])
-
-    @pl.when(step == PAIR_CHUNKS - 1)
+        for j in range(BATCH):
+            for half in range(2):
+                tile = 2 * (first + j) + half
+                mine = lane + tile * 128 >= origin
+                new = values[j * ROWS : (j + 1) * ROWS, 128 * half : 128 * half + 128]
+                line[tile] = jnp.where(mine, new, line[tile])
+
+    @pl.when(step == STEPS - 1)
     def _():
         lane = lax.broadcasted_iota(i32, (ROWS, 128), 1)
         for q in range(4):
@@ -286,27 +277,27 @@
     depth = GROUPS * TILES * devices
 
     def table_at(pair, step, lats, points):
-        total = lat_scalars(lats, points, 2 * pair)[2] + lat_scalars(lats, points, 2 * pair + 1)[2]
-        return (pair * PAIR_CHUNKS + jnp.minimum(step, total - 1), 0, 0, 0)
+        _, _, batches_a, batches = pair_batches(lats, points, pair)
+        return (2 * pair + jnp.where(jnp.minimum(step, batches - 1) >= batches_a, 1, 0), 0, 0)
 
     return pl.pallas_call(
         functools.partial(synthesis_kernel, float(truncation)),
         out_shape=jax.ShapeDtypeStruct((8, 20, QUARTER), bf16),
         grid_spec=pltpu.PrefetchScalarGridSpec(
             num_scalar_prefetch=2,
-            grid=(2, PAIR_CHUNKS),
+            grid=(2, STEPS),
             in_specs=[
                 pl.BlockSpec((devices, 4 * TILES, 128), lambda p, s, a, b: (0, 0, 0)),
                 pl.BlockSpec((1, depth), lambda p, s, a, b: (0, 0)),
                 pl.BlockSpec((GROUPS * 2 * ROWS, 128), lambda p, s, a, b: (0, 0)),
-                pl.BlockSpec((1, 2, depth, CHUNK), table_at),
+                pl.BlockSpec((1, 2 * depth, CHUNK), table_at),
             ],
             out_specs=pl.BlockSpec((4, 20, QUARTER), lambda p, s, a, b: (p, 0, 0)),
             scratch_shapes=[
                 pltpu.VMEM((devices * 4 * TILES, 128), f32),
-                pltpu.VMEM((4, 4 * ROWS, depth), bf16),
-                pltpu.VMEM((4, 4 * ROWS, depth), bf16),
-                pltpu.VMEM((44, ROWS, 128), f32),
+                pltpu.VMEM((4, 2, ROWS, depth), f32),
+                pltpu.VMEM((BATCH * ROWS, 2 * depth), bf16),
+                pltpu.VMEM((2 * (LAST + BATCH) + 2, ROWS, 128), f32),
             ],
         ),
         compiler_params=pltpu.CompilerParams(vmem_limit_bytes=32 << 20),

time: 111 us -> 87.2 us (0.79)
  Pallas kernels: 41 us -> 29.3 us
  local copies, waits for them, and re-layouts: 16.7 us -> 5.96 us
    unnamed x14 -> x10, local copies, waits for them, and re-layouts: 13.9 us -> 3.1 us
    pallas_call x1, Pallas kernels: 22.9 us -> 12.9 us  [fourier_tables(): pl.pallas_call(functools.partial(table_kernel, float(truncation)), out_sh...]
    pallas_call x1, Pallas kernels: 7.48 us -> 5.73 us  [synthesis(): pl.pallas_call(functools.partial(synthesis_kernel, float(truncation)), ou...]
  transfers between devices with their start and end apart: 2 -> 2, of which waited for: 0 -> 0; matrix products, arithmetic and copies ran while one was open for 2% -> 2% of each run, Pallas kernels for 29% -> 25%
where the time goes in v1:
time: 87.2 us; the launch traced here: 85.8 us
  Pallas kernels  29.3 us (34%)
  blocking collectives  24.5 us (28%)
  starting transfers between devices  24.3 us (28%)
  local copies, waits for them, and re-layouts  5.96 us (7%)
  other arithmetic  1.54 us (2%)
    all_to_all x1, blocking collectives, on_device(): blocks = lax.all_to_all(blocks, 'field', 0, 0, tiled=True)  24.5 us
    all_to_all x1, starting transfers between devices, on_device(): lax.all_to_all(jnp.broadcast_to(mine[None, None, :], (devices, 1, 128)),...  14 us
    pallas_call x1, Pallas kernels, fourier_tables(): pl.pallas_call(functools.partial(table_kernel, float(truncation)), out_sh...  12.9 us
    all_to_all x1, starting transfers between devices, on_device(): received = lax.all_to_all(ordered, 'wave', 0, 0, tiled=True)  10.3 us
    pallas_call x1, Pallas kernels, legendre_sums(): pl.pallas_call(functools.partial(legendre_kernel, rows - 2), out_shape=ja...  8.5 us
    pallas_call x1, Pallas kernels, synthesis(): pl.pallas_call(functools.partial(synthesis_kernel, float(truncation)), ou...  5.73 us
    unnamed x10, local copies, waits for them, and re-layouts  3.1 us
    pallas_call x1, Pallas kernels, order_latitudes(): pl.pallas_call(order_kernel, out_shape=jax.ShapeDtypeStruct((devices, 4 *...  2.18 us
  transfers between devices with their start and end apart: 2, of which 0 were waited for; matrix products, arithmetic and copies ran while one was open for 2% of the time, Pallas kernels for 25%

profile of v1, /device:TPU:6, one launch (start us, length us, event | category | flops | bytes accessed | tf_op | source)
XLA Modules:
  0.0 85.8 jit_solution(1921478164647984660)
XLA Ops:
  0.0 0.7 add_convert_fusion
  0.8 0.6 broadcast_in_dim.2
  1.4 14.0 %all-to-all-start = ((f32[64,1,128]{2,1,0:T(1,128)}), f32[64,1,128]{2,1,0:T(1,128)S(1)}, u32[]{:S(2)}, u32[]{:S(2)}) async-start(f32[64,1,128]{2,1,0:T(1,128)} %broadcast_in_dim.2), calls=%async_computation | async-start | bytes 65536 | tf_op jit(solution)/shard_map/all_to_all | solution.py:319
  15.4 8.5 %shard_map.64.sums_ref = f32[20,24,256]{2,1,0:T(8,128)} custom-call(s32[10]{0:T(128)} %waves.1, f32[10,10,2,1281]{3,2,1,0:T(2,128)} %bitcast.18, bf16[10,1281,128]{2,1,0:T(8,128)(2,1)} %leg_ref.1), custom_call_target="tpu_custom_call" | custom-call | tf_op jit(solution)/shard_map/pallas_call | solution.py:57
  23.9 0.0 all-to-all-done
  23.9 0.0 copy-start.4
  23.9 0.6 copy-done.4
  24.5 0.0 copy-start.1
  24.5 0.0 copy-start.2
  24.5 0.0 copy-start.3
  24.5 2.2 %shard_map.65 = bf16[64,16,128]{2,1,0:T(8,128)(2,1)} custom-call(f32[64,128]{1,0:T(8,128)} %bitcast.19, f32[20,24,256]{2,1,0:T(8,128)} %shard_map.64.sums_ref), custom_call_target="tpu_custom_call" | custom-call | tf_op jit(solution)/shard_map/pallas_call | solution.py:90
  26.7 10.3 %all-to-all-start.1 = ((bf16[64,16,128]{2,1,0:T(8,128)(2,1)}), bf16[64,16,128]{2,1,0:T(8,128)(2,1)S(1)}, u32[]{:S(2)}, u32[]{:S(2)}) async-start(bf16[64,16,128]{2,1,0:T(8,128)(2,1)} %shard_map.65), calls=%async_computation.1 | async-start | bytes 524288 | tf_op jit(solution)/shard_map/all_to_all | solution.py:323
  37.1 0.8 slice_bitcast_fusion
  37.8 0.1 copy.13
  37.9 0.8 fusion
  38.7 0.1 copy.14
  38.8 0.1 reshape.20.wave_ref
  38.9 12.9 %shard_map.66.table_ref = bf16[4,2560,256]{2,1,0:T(8,128)(2,1)} custom-call(s32[4]{0:T(128)} %lat_rows.3, s32[256]{0:T(256)} %npoints.3, f32[64,128]{1,0:T(8,128)} %bitcast.22), custom_call_target="tpu_custom_call" | custom-call | tf_op jit(solution)/shard_map/pallas_call | solution.py:160
  51.8 0.0 all-to-all-done.1.got_ref
  51.8 0.0 copy-done.1
  51.8 0.0 copy-done.2
  51.8 0.0 copy-done.3
  51.8 0.0 copy-start
  51.8 2.5 %copy-done = bf16[4,2560,256]{2,1,0:T(8,128)(2,1)S(1)} copy-done((bf16[4,2560,256]{2,1,0:T(8,128)(2,1)S(1)}, bf16[4,2560,256]{2,1,0:T(8,128)(2,1)}, u32[]{:S(2)}) %copy-start) | copy-done | bytes 5242904
  54.3 5.7 %shard_map.67 = bf16[8,20,1289]{2,1,0:T(8,128)(2,1)S(1)} custom-call(s32[4]{0:T(128)S(1)} %copy-done.3, s32[256]{0:T(256)S(1)} %copy-done.2, bf16[64,16,128]{2,1,0:T(8,128)(2,1)S(1)} %all-to-all-done.1.got_ref, f32[1,1280]{1,0:T(1,128)S(1)} %reshape.20.wave_ref, bf16[240,128]{1,0:T(8,128)(2,1)S(1)} %copy-done.1, bf16[4,2560,256]{2,1,0:T(8,128)(2,1)S(1)} %copy-done), custom_call_target="tpu_custom_call" | custom-call | tf_op jit(solution)/shard_map/pallas_call | solution.py:283
  60.0 24.5 %all_to_all.15 = bf16[8,20,1289]{2,1,0:T(8,128)(2,1)S(1)} all-to-all(bf16[8,20,1289]{2,1,0:T(8,128)(2,1)S(1)} %shard_map.67), channel_id=1, replica_groups=mesh['wave'=64,'field'=8] {'field'}, dimensions={0} | all-to-all | bytes 824960 | tf_op jit(solution)/shard_map/all_to_all | solution.py:327
  84.6 0.3 copy.17
  85.0 0.8 copy.18
  (5 shorter events, 0.1 us)
Async XLA Ops:
  1.4 22.5 %all-to-all-start = ((f32[64,1,128]{2,1,0:T(1,128)}), f32[64,1,128]{2,1,0:T(1,128)S(1)}, u32[]{:S(2)}, u32[]{:S(2)}) async-start(f32[64,1,128]{2,1,0:T(1,128)} %broadcast_in_dim.2), calls=%async_computation | async-start | bytes 65536 | tf_op jit(solution)/shard_map/all_to_all | solution.py:319
  23.9 0.6 copy-start.4
  24.5 27.2 %copy-start.1 = (bf16[240,128]{1,0:T(8,128)(2,1)S(1)}, bf16[240,128]{1,0:T(8,128)(2,1)}, u32[]{:S(2)}) copy-start(bf16[240,128]{1,0:T(8,128)(2,1)} %constant.7.clone.select_ref) | copy-start | bytes 184324
  24.5 27.2 %copy-start.2 = (s32[256]{0:T(256)S(1)}, s32[256]{0:T(256)}, u32[]{:S(2)}) copy-start(s32[256]{0:T(256)} %npoints.3) | copy-start | bytes 3076
  24.5 27.2 %copy-start.3 = (s32[4]{0:T(128)S(1)}, s32[4]{0:T(128)}, u32[]{:S(2)}) copy-start(s32[4]{0:T(128)} %lat_rows.3) | copy-start | bytes 52
  26.7 25.1 %all-to-all-start.1 = ((bf16[64,16,128]{2,1,0:T(8,128)(2,1)}), bf16[64,16,128]{2,1,0:T(8,128)(2,1)S(1)}, u32[]{:S(2)}, u32[]{:S(2)}) async-start(bf16[64,16,128]{2,1,0:T(8,128)(2,1)} %shard_map.65), calls=%async_computation.1 | async-start | bytes 524288 | tf_op jit(solution)/shard_map/all_to_all | solution.py:323
  51.8 2.5 %copy-start = (bf16[4,2560,256]{2,1,0:T(8,128)(2,1)S(1)}, bf16[4,2560,256]{2,1,0:T(8,128)(2,1)}, u32[]{:S(2)}) copy-start(bf16[4,2560,256]{2,1,0:T(8,128)(2,1)} %shard_map.66.table_ref) | copy-start | bytes 15728644

commit v2 on v1

--- a/solution.py
+++ b/solution.py
@@ -14,8 +14,8 @@
 GROUPS = 5
 TILES = 4
 ROWS = 24
-SIN = (6.283184905907144, -41.34158660945749, 81.59984497508991, -76.61321302879018, 41.33641025544816, -12.459753683550199)
-COS = (0.999999988711474, -19.739204378854772, 64.93911099976975, -85.4500154366872, 60.16656814312298, -25.963448256110482, 6.5226306139218035)
+SIN = (6.283184915155849, -41.3415888250942, 81.59992747560547, -76.6142661520567, 41.34181133252104, -12.469328879159221)
+COS = (0.9999992080920543, -19.73897953618229, 64.92862553583919, -85.27120644254374, 58.78833787867872, -21.067254412050286)
 f32, bf16, i32 = jnp.float32, jnp.bfloat16, jnp.int32
 
 
@@ -90,8 +90,9 @@
     return pl.pallas_call(
         order_kernel,
         out_shape=jax.ShapeDtypeStruct((devices, 4 * TILES, 128), bf16),
-        in_specs=[pl.BlockSpec(memory_space=pltpu.VMEM)] * 2,
-        out_specs=pl.BlockSpec(memory_space=pltpu.VMEM),
+        grid=(1,),
+        in_specs=[pl.BlockSpec(index.shape, lambda i: (0, 0)), pl.BlockSpec(sums.shape, lambda i: (0, 0, 0))],
+        out_specs=pl.BlockSpec((devices, 4 * TILES, 128), lambda i: (0, 0, 0)),
         scratch_shapes=[pltpu.VMEM((devices * 4 * TILES, 128), f32)],
     )(index, sums)
 
@@ -110,7 +111,7 @@
     return poly(COS, y), poly(SIN, y) * f
 
 
-BLOCK = 64
+BLOCK = 128
 
 
 def table_kernel(truncation, lat_rows, npoints, index_ref, out_ref, waves):
@@ -129,26 +130,16 @@
                 at = devices * (TILES * g + t)
                 waves[at : at + devices, :] = jnp.broadcast_to(column, (devices, 128))
 
-    lane = lax.broadcasted_iota(i32, (BLOCK, 128), 1).astype(f32)
-    n = jnp.full((8, 128), npoints[lat_rows[l]], i32).astype(f32)
-    inverse = 1.0 / n
-    n, inverse = n[0:1], inverse[0:1]
+    odd = (2 * lax.broadcasted_iota(i32, (BLOCK, 128), 1) + 1).astype(f32)
+    n = jnp.full((8, 128), 2 * npoints[lat_rows[l]], i32).astype(f32)
+    inverse = (1.0 / n)[0:1]
+    n = n[0:1]
 
     def rows_block(r, carry):
         at = pl.multiple_of(r * BLOCK, BLOCK)
-        k = waves[pl.ds(at, BLOCK), :]
-        real, imag = sincos(k * lane, n, inverse)
-        c64 = jnp.broadcast_to(real[:, 64:65], (BLOCK, 128))
-        s64 = jnp.broadcast_to(imag[:, 64:65], (BLOCK, 128))
-        c128 = 2.0 * c64 * c64 - 1.0
-        s128 = 2.0 * c64 * s64
-        scale = jnp.where(2.0 * k < n, jnp.where(k == 0.0, 1.0, 2.0), 0.0)
-        real = real * scale
-        imag = imag * scale
-        out_ref[0, pl.ds(at, BLOCK), 0:128] = real.astype(bf16)
-        out_ref[0, pl.ds(at, BLOCK), 128:256] = (real * c128 - imag * s128).astype(bf16)
-        out_ref[0, pl.ds(depth + at, BLOCK), 0:128] = (-imag).astype(bf16)
-        out_ref[0, pl.ds(depth + at, BLOCK), 128:256] = (-imag * c128 - real * s128).astype(bf16)
+        cosine, sine = sincos(waves[pl.ds(at, BLOCK), :] * odd, n, inverse)
+        out_ref[0, pl.ds(at, BLOCK), :] = cosine.astype(bf16)
+        out_ref[0, pl.ds(depth + at, BLOCK), :] = sine.astype(bf16)
         return carry
 
     lax.fori_loop(0, depth // BLOCK, rows_block, 0)
@@ -159,12 +150,12 @@
     depth = GROUPS * TILES * devices
     return pl.pallas_call(
         functools.partial(table_kernel, float(truncation)),
-        out_shape=jax.ShapeDtypeStruct((4, 2 * depth, CHUNK), bf16),
+        out_shape=jax.ShapeDtypeStruct((4, 2 * depth, CHUNK // 2), bf16),
         grid_spec=pltpu.PrefetchScalarGridSpec(
             num_scalar_prefetch=2,
             grid=(4,),
             in_specs=[pl.BlockSpec((devices, 128), lambda l, a, b: (0, 0))],
-            out_specs=pl.BlockSpec((1, 2 * depth, CHUNK), lambda l, a, b: (l, 0, 0)),
+            out_specs=pl.BlockSpec((1, 2 * depth, CHUNK // 2), lambda l, a, b: (l, 0, 0)),
             scratch_shapes=[pltpu.VMEM((depth, 128), f32)],
         ),
     )(lat_rows, npoints, index)
@@ -183,7 +174,7 @@
     return n_a, start_b, batches_a, batches_a + batches_b
 
 
-def synthesis_kernel(truncation, lat_rows, npoints, got_ref, wave_ref, select_ref, table_ref, out_ref, got, parts, left, line):
+def synthesis_kernel(truncation, lat_rows, npoints, got_ref, wave_ref, select_ref, reverse_ref, table_ref, out_ref, got, parts, left, line):
     pair, step = pl.program_id(0), pl.program_id(1)
     devices = got_ref.shape[0]
     rows = TILES * devices
@@ -214,15 +205,17 @@
 
     @pl.when(step < batches)
     def _():
-        n = jnp.full((8, 128), npoints[lat_rows[l]], i32).astype(f32)
+        n = jnp.full((8, 128), 2 * npoints[lat_rows[l]], i32).astype(f32)
         inverse = (1.0 / n)[0:1, 0:1]
         n = n[0:1, 0:1]
         chunk = lax.broadcasted_iota(i32, (BATCH, rows), 0)
-        t0 = ((first + chunk) * CHUNK - origin).astype(f32)
+        center = (2 * CHUNK * (first + chunk) - 2 * origin + CHUNK - 1).astype(f32)
         for g in range(GROUPS):
             at = slice(g * rows, (g + 1) * rows)
             k = wave_ref[:, at]
-            cosine, sine = sincos(t0 * k, n, inverse)
+            weight = jnp.where(4.0 * k < n, jnp.where(k == 0.0, 1.0, 2.0), 0.0)
+            cosine, sine = sincos(center * k, n, inverse)
+            cosine, sine = cosine * weight, sine * weight
             real, imag = parts[l, 0, :, at], parts[l, 1, :, at]
             for j in range(0, BATCH, 2):
                 turned = [
@@ -233,14 +226,16 @@
                 left[to, at] = jnp.concatenate([turned[0][0], turned[1][0]], axis=0).astype(bf16)
                 at_imag = slice(depth + g * rows, depth + (g + 1) * rows)
                 left[to, at_imag] = jnp.concatenate([turned[0][1], turned[1][1]], axis=0).astype(bf16)
-        values = jnp.dot(left[...], table_ref[0], preferred_element_type=f32)
+        even = jnp.dot(left[:, 0:depth], table_ref[0, 0:depth], preferred_element_type=f32)
+        odd = jnp.dot(left[:, depth : 2 * depth], table_ref[0, depth : 2 * depth], preferred_element_type=f32)
+        before = jnp.dot((even + odd).astype(bf16), reverse_ref[...], preferred_element_type=f32)
+        after = even - odd
         lane = lax.broadcasted_iota(i32, (ROWS, 128), 1)
         for j in range(BATCH):
-            for half in range(2):
+            for half, values in ((0, before), (1, after)):
                 tile = 2 * (first + j) + half
                 mine = lane + tile * 128 >= origin
-                new = values[j * ROWS : (j + 1) * ROWS, 128 * half : 128 * half + 128]
-                line[tile] = jnp.where(mine, new, line[tile])
+                line[tile] = jnp.where(mine, values[j * ROWS : (j + 1) * ROWS], line[tile])
 
     @pl.when(step == STEPS - 1)
     def _():
@@ -276,6 +271,8 @@
     devices = received.shape[0]
     depth = GROUPS * TILES * devices
 
+    reverse = np.eye(128)[::-1].astype(jnp.bfloat16)
+
     def table_at(pair, step, lats, points):
         _, _, batches_a, batches = pair_batches(lats, points, pair)
         return (2 * pair + jnp.where(jnp.minimum(step, batches - 1) >= batches_a, 1, 0), 0, 0)
@@ -290,7 +287,8 @@
                 pl.BlockSpec((devices, 4 * TILES, 128), lambda p, s, a, b: (0, 0, 0)),
                 pl.BlockSpec((1, depth), lambda p, s, a, b: (0, 0)),
                 pl.BlockSpec((GROUPS * 2 * ROWS, 128), lambda p, s, a, b: (0, 0)),
-                pl.BlockSpec((1, 2 * depth, CHUNK), table_at),
+                pl.BlockSpec((128, 128), lambda p, s, a, b: (0, 0)),
+                pl.BlockSpec((1, 2 * depth, CHUNK // 2), table_at),
             ],
             out_specs=pl.BlockSpec((4, 20, QUARTER), lambda p, s, a, b: (p, 0, 0)),
             scratch_shapes=[
@@ -301,7 +299,7 @@
             ],
         ),
         compiler_params=pltpu.CompilerParams(vmem_limit_bytes=32 << 20),
-    )(lat_rows, npoints, received, wave_line, select_rows(), tables)
+    )(lat_rows, npoints, received, wave_line, select_rows(), reverse, tables)
 
 
 def wave_line_of(index, truncation):
@@ -322,6 +320,7 @@
     ordered = order_latitudes(index, sums)
     received = lax.all_to_all(ordered, "wave", 0, 0, tiled=True)
     tables = fourier_tables(lat_rows, npoints, index, truncation)
+    tables = pltpu.with_memory_space_constraint(tables, pltpu.HBM)
     wave_line = wave_line_of(index, float(truncation))
     blocks = synthesis(lat_rows, npoints, received, wave_line, tables, truncation)
     blocks = lax.all_to_all(blocks, "field", 0, 0, tiled=True)

time: 87.2 us -> 84.9 us (0.974)
  Pallas kernels: 29.3 us -> 23.7 us
  waiting for transfers between devices: 0.01 us -> 4.12 us
  local copies, waits for them, and re-layouts: 5.96 us -> 3.48 us
  blocking collectives: 24.5 us -> 26.2 us
    pallas_call x1, Pallas kernels: 12.9 us -> 5.61 us  [fourier_tables(): pl.pallas_call(functools.partial(table_kernel, float(truncation)), out_sh...]
    all_to_all x1, waiting for transfers between devices: 0.01 us -> 4.12 us  [on_device(): received = lax.all_to_all(ordered, 'wave', 0, 0, tiled=True)]
    unnamed x10, local copies, waits for them, and re-layouts: 3.1 us -> 0.62 us
    pallas_call x1, Pallas kernels: 5.73 us -> 7.43 us  [synthesis(): pl.pallas_call(functools.partial(synthesis_kernel, float(truncation)), ou...]
    all_to_all x1, blocking collectives: 24.5 us -> 26.2 us  [on_device(): blocks = lax.all_to_all(blocks, 'field', 0, 0, tiled=True)]
  transfers between devices with their start and end apart: 2 -> 2, of which waited for: 0 -> 1; matrix products, arithmetic and copies ran while one was open for 2% -> 2% of each run, Pallas kernels for 25% -> 17%
where the time goes in v2:
time: 84.9 us; the launch traced here: 83.5 us
  blocking collectives  26.2 us (31%)
  starting transfers between devices  24.3 us (29%)
  Pallas kernels  23.7 us (28%)
  waiting for transfers between devices  4.12 us (5%)
  local copies, waits for them, and re-layouts  3.48 us (4%)
  other arithmetic  1.54 us (2%)
    all_to_all x1, blocking collectives, on_device(): blocks = lax.all_to_all(blocks, 'field', 0, 0, tiled=True)  26.2 us
    all_to_all x1, starting transfers between devices, on_device(): lax.all_to_all(jnp.broadcast_to(mine[None, None, :], (devices, 1, 128)),...  14 us
    all_to_all x1, starting transfers between devices, on_device(): received = lax.all_to_all(ordered, 'wave', 0, 0, tiled=True)  10.3 us
    pallas_call x1, Pallas kernels, legendre_sums(): pl.pallas_call(functools.partial(legendre_kernel, rows - 2), out_shape=ja...  8.5 us
    pallas_call x1, Pallas kernels, synthesis(): pl.pallas_call(functools.partial(synthesis_kernel, float(truncation)), ou...  7.43 us
    pallas_call x1, Pallas kernels, fourier_tables(): pl.pallas_call(functools.partial(table_kernel, float(truncation)), out_sh...  5.61 us
    all_to_all x1, waiting for transfers between devices, on_device(): received = lax.all_to_all(ordered, 'wave', 0, 0, tiled=True)  4.12 us
    pallas_call x1, Pallas kernels, order_latitudes(): pl.pallas_call(order_kernel, out_shape=jax.ShapeDtypeStruct((devices, 4 *...  2.17 us
  transfers between devices with their start and end apart: 2, of which 1 were waited for; matrix products, arithmetic and copies ran while one was open for 2% of the time, Pallas kernels for 17%

profile of v2, /device:TPU:6, one launch (start us, length us, event | category | flops | bytes accessed | tf_op | source)
XLA Modules:
  0.0 83.5 jit_solution(8371234881488553465)
XLA Ops:
  0.0 0.7 add_convert_fusion
  0.8 0.6 broadcast_in_dim.2
  1.4 14.0 %all-to-all-start = ((f32[64,1,128]{2,1,0:T(1,128)}), f32[64,1,128]{2,1,0:T(1,128)S(1)}, u32[]{:S(2)}, u32[]{:S(2)}) async-start(f32[64,1,128]{2,1,0:T(1,128)} %broadcast_in_dim.2), calls=%async_computation | async-start | bytes 65536 | tf_op jit(solution)/shard_map/all_to_all | solution.py:317
  15.4 8.5 %shard_map.73.sums_ref = f32[20,24,256]{2,1,0:T(8,128)} custom-call(s32[10]{0:T(128)} %waves.1, f32[10,10,2,1281]{3,2,1,0:T(2,128)} %bitcast.18, bf16[10,1281,128]{2,1,0:T(8,128)(2,1)} %leg_ref.1), custom_call_target="tpu_custom_call" | custom-call | tf_op jit(solution)/shard_map/pallas_call | solution.py:57
  23.9 0.0 copy-start
  23.9 0.0 copy-start.1
  23.9 0.0 copy-start.2
  23.9 0.0 copy-start.3
  23.9 0.0 all-to-all-done
  23.9 0.0 copy-start.4
  24.0 0.6 copy-done.4
  24.6 2.2 %shard_map.74 = bf16[64,16,128]{2,1,0:T(8,128)(2,1)} custom-call(f32[64,128]{1,0:T(8,128)} %bitcast.19, f32[20,24,256]{2,1,0:T(8,128)} %shard_map.73.sums_ref), custom_call_target="tpu_custom_call" | custom-call | tf_op jit(solution)/shard_map/pallas_call | solution.py:90
  26.7 10.3 %all-to-all-start.1 = ((bf16[64,16,128]{2,1,0:T(8,128)(2,1)}), bf16[64,16,128]{2,1,0:T(8,128)(2,1)S(1)}, u32[]{:S(2)}, u32[]{:S(2)}) async-start(bf16[64,16,128]{2,1,0:T(8,128)(2,1)} %shard_map.74), calls=%async_computation.1 | async-start | bytes 524288 | tf_op jit(solution)/shard_map/all_to_all | solution.py:321
  37.1 0.8 slice_bitcast_fusion
  37.8 0.1 copy.14
  37.9 0.8 fusion
  38.7 0.1 copy.15
  38.8 0.1 reshape.20.wave_ref
  38.9 5.6 %shard_map.75.table_ref = bf16[4,2560,128]{2,1,0:T(8,128)(2,1)} custom-call(s32[4]{0:T(128)} %lat_rows.3, s32[256]{0:T(256)} %npoints.3, f32[64,128]{1,0:T(8,128)} %bitcast.22), custom_call_target="tpu_custom_call" | custom-call | tf_op jit(solution)/shard_map/pallas_call | solution.py:151
  44.5 4.1 %all-to-all-done.1.got_ref = bf16[64,16,128]{2,1,0:T(8,128)(2,1)S(1)} async-done(((bf16[64,16,128]{2,1,0:T(8,128)(2,1)}), bf16[64,16,128]{2,1,0:T(8,128)(2,1)S(1)}, u32[]{:S(2)}, u32[]{:S(2)}) %all-to-all-start.1) | async-done | bytes 262176 | tf_op jit(solution)/shard_map/all_to_all | solution.py:321
  48.6 0.0 copy-done
  48.6 0.0 copy-done.1
  48.6 0.0 copy-done.2
  48.6 0.0 copy-done.3
  48.6 7.4 %shard_map.76 = bf16[8,20,1289]{2,1,0:T(8,128)(2,1)S(1)} custom-call(s32[4]{0:T(128)S(1)} %copy-done.3, s32[256]{0:T(256)S(1)} %copy-done.2, bf16[64,16,128]{2,1,0:T(8,128)(2,1)S(1)} %all-to-all-done.1.got_ref, f32[1,1280]{1,0:T(1,128)S(1)} %reshape.20.wave_ref, bf16[240,128]{1,0:T(8,128)(2,1)S(1)} %copy-done, bf16[128,128]{1,0:T(8,128)(2,1)S(1)} %copy-done.1, ...), custom_call_target="tpu_custom_call" | custom-call | tf_op jit(solution)/shard_map/pallas_call | solution.py:280
  56.1 26.2 %all_to_all.15 = bf16[8,20,1289]{2,1,0:T(8,128)(2,1)S(1)} all-to-all(bf16[8,20,1289]{2,1,0:T(8,128)(2,1)S(1)} %shard_map.76), channel_id=1, replica_groups=mesh['wave'=64,'field'=8] {'field'}, dimensions={0} | all-to-all | bytes 824960 | tf_op jit(solution)/shard_map/all_to_all | solution.py:326
  82.3 0.3 copy.18
  82.6 0.8 copy.19
  (5 shorter events, 0.1 us)
Async XLA Ops:
  1.4 22.6 %all-to-all-start = ((f32[64,1,128]{2,1,0:T(1,128)}), f32[64,1,128]{2,1,0:T(1,128)S(1)}, u32[]{:S(2)}, u32[]{:S(2)}) async-start(f32[64,1,128]{2,1,0:T(1,128)} %broadcast_in_dim.2), calls=%async_computation | async-start | bytes 65536 | tf_op jit(solution)/shard_map/all_to_all | solution.py:317
  23.9 24.7 %copy-start = (bf16[240,128]{1,0:T(8,128)(2,1)S(1)}, bf16[240,128]{1,0:T(8,128)(2,1)}, u32[]{:S(2)}) copy-start(bf16[240,128]{1,0:T(8,128)(2,1)} %constant.9.clone.select_ref) | copy-start | bytes 184324
  23.9 24.7 %copy-start.1 = (bf16[128,128]{1,0:T(8,128)(2,1)S(1)}, bf16[128,128]{1,0:T(8,128)(2,1)}, u32[]{:S(2)}) copy-start(bf16[128,128]{1,0:T(8,128)(2,1)} %constant.10.clone.reverse_ref) | copy-start | bytes 98308
  23.9 24.7 %copy-start.2 = (s32[256]{0:T(256)S(1)}, s32[256]{0:T(256)}, u32[]{:S(2)}) copy-start(s32[256]{0:T(256)} %npoints.3) | copy-start | bytes 3076
  23.9 24.7 %copy-start.3 = (s32[4]{0:T(128)S(1)}, s32[4]{0:T(128)}, u32[]{:S(2)}) copy-start(s32[4]{0:T(128)} %lat_rows.3) | copy-start | bytes 52
  23.9 0.6 copy-start.4
  26.7 21.9 %all-to-all-start.1 = ((bf16[64,16,128]{2,1,0:T(8,128)(2,1)}), bf16[64,16,128]{2,1,0:T(8,128)(2,1)S(1)}, u32[]{:S(2)}, u32[]{:S(2)}) async-start(bf16[64,16,128]{2,1,0:T(8,128)(2,1)} %shard_map.74), calls=%async_computation.1 | async-start | bytes 524288 | tf_op jit(solution)/shard_map/all_to_all | solution.py:321

commit v3 on v2

v3 whole, which is shorter than its diff:
```python
import functools

import jax
import jax.numpy as jnp
import numpy as np
from jax import lax
from jax.experimental import pallas as pl
from jax.experimental.pallas import tpu as pltpu
from jax.sharding import PartitionSpec as P

ROW_PAIR = 5156
QUARTER = ROW_PAIR // 4
CHUNK = 256
GROUPS = 5
TILES = 4
ROWS = 24
SIN = (6.283184915155849, -41.3415888250942, 81.59992747560547, -76.6142661520567, 41.34181133252104, -12.469328879159221)
COS = (0.9999992080920543, -19.73897953618229, 64.92862553583919, -85.27120644254374, 58.78833787867872, -21.067254412050286)
f32, bf16, i32 = jnp.float32, jnp.bfloat16, jnp.int32
VMEM_SPEC = pl.BlockSpec(memory_space=pltpu.VMEM)


def legendre_kernel(truncation, waves, spec_ref, leg_ref, out_ref, coeffs):
    slot = pl.program_id(0)
    rows = truncation + 2
    fields = spec_ref.shape[1]

    @pl.when(slot == 0)
    def _():
        coeffs[...] = jnp.zeros_like(coeffs)

    for field in range(fields):
        coeffs[2 * field : 2 * field + 2, 0:rows] = spec_ref[0, field]
    split = truncation + 1 - waves[slot]
    row = lax.broadcasted_iota(i32, (1, rows), 1)
    low = row < split
    offset = jnp.where(low, row, row - split)
    sign = jnp.where(offset % 2 == 0, 1.0, -1.0).astype(f32)
    low = jnp.where(low, 1.0, 0.0).astype(f32)
    high = 1.0 - low
    values = coeffs[:, 0:rows]
    stacked = jnp.concatenate([values * mask for mask in (low, low * sign, high, high * sign)], axis=0)
    stacked = stacked.astype(bf16)
    main = rows - 1
    sums = jnp.dot(stacked[:, 0:main], leg_ref[0, 0:main, :], preferred_element_type=f32)
    last = stacked[:, main:rows].astype(f32) * leg_ref[0, main:rows, :].astype(f32)
    sums = sums + last
    for half in range(2):
        for side in range(2):
            at = (2 * half + side) * ROWS
            out_ref[half, :, 128 * side : 128 * side + 128] = sums[at : at + ROWS, :]


def legendre_sums(wave_pairs, spectral, legendre):
    slots, rows, northern = legendre.shape
    fields = spectral.shape[3]
    parts = pltpu.with_memory_space_constraint(jnp.transpose(spectral, (0, 3, 2, 1)), pltpu.HBM)
    legendre = pltpu.with_memory_space_constraint(legendre, pltpu.HBM)
    return pl.pallas_call(
        functools.partial(legendre_kernel, rows - 2),
        out_shape=pltpu.VMEM((2 * slots, ROWS, 2 * northern), f32),
        grid_spec=pltpu.PrefetchScalarGridSpec(
            num_scalar_prefetch=1,
            grid=(slots,),
            in_specs=[
                pl.BlockSpec((1, fields, 2, rows), lambda p, w: (p, 0, 0, 0)),
                pl.BlockSpec((1, rows, northern), lambda p, w: (p, 0, 0)),
            ],
            out_specs=pl.BlockSpec((2, ROWS, 2 * northern), lambda p, w: (p, 0, 0)),
            scratch_shapes=[pltpu.VMEM((ROWS, 1408), f32)],
        ),
        compiler_params=pltpu.CompilerParams(vmem_limit_bytes=8 << 20),
    )(wave_pairs, parts, legendre)


def order_kernel(index_ref, sums_ref, out_ref, scratch):
    devices, lats = index_ref.shape[0], sums_ref.shape[2]
    index = index_ref[:, 0, :]
    lane = lax.broadcasted_iota(i32, (devices, lats), 1).astype(f32)
    onehot = jnp.concatenate(
        [jnp.where(index[:, 10 + j : 11 + j] == lane, 1.0, 0.0) for j in range(4)], axis=0
    ).astype(bf16)
    for t in range(TILES):
        part = sums_ref[GROUPS * t : GROUPS * (t + 1)].reshape(GROUPS * ROWS, lats)
        part = jnp.concatenate([part, jnp.zeros((128 - GROUPS * ROWS, lats), f32)], axis=0).astype(bf16)
        picked = lax.dot_general(onehot, part, (((1,), (1,)), ((), ())), preferred_element_type=f32)
        for j in range(4):
            scratch[pl.ds(j * TILES + t, devices, 4 * TILES), :] = picked[devices * j : devices * (j + 1), :]
    out_ref[...] = scratch[...].reshape(out_ref.shape).astype(bf16)


def order_latitudes(index, sums):
    devices = index.shape[0]
    return pl.pallas_call(
        order_kernel,
        out_shape=jax.ShapeDtypeStruct((devices, 4 * TILES, 128), bf16),
        in_specs=[VMEM_SPEC] * 2,
        out_specs=VMEM_SPEC,
        scratch_shapes=[pltpu.VMEM((devices * 4 * TILES, 128), f32)],
        compiler_params=pltpu.CompilerParams(vmem_limit_bytes=8 << 20),
    )(index, sums)


def poly(coefficients, y):
    total = jnp.full_like(y, coefficients[-1])
    for c in coefficients[-2::-1]:
        total = total * y + c
    return total


def sincos(product, n, inverse):
    turns = jnp.floor(product * inverse + 0.5)
    f = (product - turns * n) * inverse
    y = f * f
    return poly(COS, y), poly(SIN, y) * f


BLOCK = 128


def table_kernel(truncation, lat_rows, npoints, index_ref, out_ref, waves):
    l = pl.program_id(0)
    devices = index_ref.shape[0]
    depth = GROUPS * TILES * devices

    @pl.when(l == 0)
    def _():
        index = index_ref[:, 0, :]
        for g in range(GROUPS):
            for t in range(TILES):
                ph = GROUPS * t + g
                column = index[:, ph // 2 : ph // 2 + 1]
                if ph % 2:
                    column = truncation - column
                at = devices * (TILES * g + t)
                waves[at : at + devices, :] = jnp.broadcast_to(column, (devices, 128))

    odd = (2 * lax.broadcasted_iota(i32, (BLOCK, 128), 1) + 1).astype(f32)
    n = jnp.full((8, 128), 2 * npoints[lat_rows[l]], i32).astype(f32)
    inverse = (1.0 / n)[0:1]
    n = n[0:1]

    def rows_block(r, carry):
        at = pl.multiple_of(r * BLOCK, BLOCK)
        cosine, sine = sincos(waves[pl.ds(at, BLOCK), :] * odd, n, inverse)
        out_ref[0, pl.ds(at, BLOCK), :] = cosine.astype(bf16)
        out_ref[0, pl.ds(depth + at, BLOCK), :] = sine.astype(bf16)
        return carry

    lax.fori_loop(0, depth // BLOCK, rows_block, 0)


def fourier_tables(lat_rows, npoints, index, truncation):
    devices = index.shape[0]
    depth = GROUPS * TILES * devices
    return pl.pallas_call(
        functools.partial(table_kernel, float(truncation)),
        out_shape=pltpu.VMEM((4, 2 * depth, CHUNK // 2), bf16),
        grid_spec=pltpu.PrefetchScalarGridSpec(
            num_scalar_prefetch=2,
            grid=(4,),
            in_specs=[VMEM_SPEC],
            out_specs=pl.BlockSpec((1, 2 * depth, CHUNK // 2), lambda l, a, b: (l, 0, 0)),
            scratch_shapes=[pltpu.VMEM((depth, 128), f32)],
        ),
        compiler_params=pltpu.CompilerParams(vmem_limit_bytes=8 << 20),
    )(lat_rows, npoints, index)


BATCH = 8
LAST = ROW_PAIR // CHUNK
WIDTH = 128
DENSE = 208
REST = QUARTER - 10 * WIDTH


def synthesis_kernel(
    truncation, lat_rows, npoints, got_ref, wave_ref, select_ref, reverse_ref, table_ref, out_ref, got, parts, left, line, dense
):
    devices = got_ref.shape[0]
    rows = TILES * devices
    depth = GROUPS * rows
    lane = lax.broadcasted_iota(i32, (ROWS, WIDTH), 1)
    got[...] = got_ref[...].reshape(devices * 4 * TILES, WIDTH).astype(f32)
    for l in range(4):
        stacked = jnp.concatenate(
            [got[pl.ds(l * TILES + t, devices, 4 * TILES), :] for t in range(TILES)], axis=0
        ).astype(bf16)
        both = lax.dot_general(select_ref[...], stacked, (((1,), (1,)), ((), ())), preferred_element_type=f32)
        for g in range(GROUPS):
            k = wave_ref[:, g * rows : (g + 1) * rows]
            row = lax.broadcasted_iota(i32, (ROWS, rows), 0)
            scale = jnp.where(row < 10, 1.0, jnp.broadcast_to(k / truncation, (ROWS, rows)))
            at = 2 * ROWS * g
            for c in range(2):
                part = both[at + c * ROWS : at + (c + 1) * ROWS] * scale
                parts[l, c, :, g * rows : (g + 1) * rows] = part.astype(bf16).astype(f32)

    def batch(l, first, origin):
        n = jnp.full((8, WIDTH), 2 * npoints[lat_rows[l]], i32).astype(f32)
        inverse = (1.0 / n)[0:1, 0:1]
        n = n[0:1, 0:1]
        chunk = lax.broadcasted_iota(i32, (BATCH, rows), 0)
        center = (2 * CHUNK * (first + chunk) - 2 * origin + CHUNK - 1).astype(f32)
        for g in range(GROUPS):
            at = slice(g * rows, (g + 1) * rows)
            at_imag = slice(depth + g * rows, depth + (g + 1) * rows)
            k = wave_ref[:, at]
            weight = jnp.where(4.0 * k < n, jnp.where(k == 0.0, 1.0, 2.0), 0.0)
            cosine, sine = sincos(center * k, n, inverse)
            cosine, sine = cosine * weight, sine * weight
            real, imag = parts[l, 0, :, at], parts[l, 1, :, at]
            for j in range(0, BATCH, 2):
                turned = [
                    (real * cosine[i : i + 1] - imag * sine[i : i + 1], imag * cosine[i : i + 1] + real * sine[i : i + 1])
                    for i in (j, j + 1)
                ]
                to = slice(j * ROWS, (j + 2) * ROWS)
                left[to, at] = jnp.concatenate([turned[0][0], turned[1][0]], axis=0).astype(bf16)
                left[to, at_imag] = jnp.concatenate([turned[0][1], turned[1][1]], axis=0).astype(bf16)
        even = jnp.dot(left[:, 0:depth], table_ref[l, 0:depth], preferred_element_type=f32)
        odd = jnp.dot(left[:, depth : 2 * depth], table_ref[l, depth : 2 * depth], preferred_element_type=f32)
        before, after = even + odd, even - odd
        for j in range(BATCH):
            tile = 2 * (first + j)
            at = slice(j * ROWS, (j + 1) * ROWS)
            line[tile] = jnp.where(WIDTH - 1 - lane + tile * WIDTH >= origin, before[at], line[tile])
            line[tile + 1] = jnp.where(lane + (tile + 1) * WIDTH >= origin, after[at], line[tile + 1])

    for pair in range(2):
        n_a = npoints[lat_rows[2 * pair]]
        start_b = lax.shift_right_arithmetic(n_a, 8)
        batches_a = lax.shift_right_arithmetic(lax.shift_right_arithmetic(n_a - 1, 8) + BATCH, 3)
        batches_b = lax.shift_right_arithmetic(LAST - start_b + BATCH, 3)

        def body(step, carry):
            second = step >= batches_a
            l = 2 * pair + jnp.where(second, 1, 0)
            first = jnp.where(second, start_b + BATCH * (step - batches_a), BATCH * step)
            batch(l, first, jnp.where(second, n_a, 0))
            return carry

        lax.fori_loop(0, batches_a + batches_b, body, 0)
        before = jnp.concatenate([line[2 * i] for i in range(LAST + 1)], axis=0).astype(bf16)
        before = jnp.dot(before, reverse_ref[...], preferred_element_type=f32)
        for i in range(LAST + 1):
            line[2 * i] = before[i * ROWS : (i + 1) * ROWS]
        for q in range(4):
            shift = (QUARTER * q) % WIDTH
            for i in range(QUARTER // WIDTH + 1):
                tile = QUARTER * q // WIDTH + i
                v = line[tile]
                if shift:
                    v = jnp.where(
                        lane < WIDTH - shift,
                        pltpu.roll(v, WIDTH - shift, 1),
                        pltpu.roll(line[tile + 1], WIDTH - shift, 1),
                    )
                if i < 10:
                    dense[q, 20 * i : 20 * i + 20] = v[0:20]
                else:
                    spread = lane[0:8]
                    dense[q, 200:208] = jnp.where(
                        spread < 16, v[0:8], jnp.where(spread < 32, pltpu.roll(v[8:16], 16, 1), pltpu.roll(v[16:24], 32, 1))
                    )
            out_ref[4 * pair + q] = dense[q].astype(bf16)


def select_rows():
    table = np.zeros((GROUPS, 2 * ROWS, 128), np.float32)
    for g in range(GROUPS):
        for f in range(10):
            real, imag = g * ROWS + 2 * f, g * ROWS + 2 * f + 1
            table[g, f, real] = 1.0
            table[g, 10 + f, imag] = -1.0
            table[g, ROWS + f, imag] = 1.0
            table[g, ROWS + 10 + f, real] = 1.0
    return table.reshape(GROUPS * 2 * ROWS, 128).astype(jnp.bfloat16)


def synthesis(lat_rows, npoints, received, wave_line, tables, truncation):
    devices = received.shape[0]
    depth = GROUPS * TILES * devices
    reverse = np.eye(WIDTH)[::-1].astype(jnp.bfloat16)
    return pl.pallas_call(
        functools.partial(synthesis_kernel, float(truncation)),
        out_shape=jax.ShapeDtypeStruct((8, DENSE, WIDTH), bf16),
        in_specs=[pl.BlockSpec(memory_space=pltpu.SMEM)] * 2 + [VMEM_SPEC] * 5,
        out_specs=VMEM_SPEC,
        scratch_shapes=[
            pltpu.VMEM((devices * 4 * TILES, WIDTH), f32),
            pltpu.VMEM((4, 2, ROWS, depth), f32),
            pltpu.VMEM((BATCH * ROWS, 2 * depth), bf16),
            pltpu.VMEM((2 * (LAST + BATCH) + 2, ROWS, WIDTH), f32),
            pltpu.VMEM((4, DENSE, WIDTH), f32),
        ],
        compiler_params=pltpu.CompilerParams(vmem_limit_bytes=16 << 20),
    )(lat_rows, npoints, received, wave_line, select_rows(), reverse, tables)


def place_kernel(in_ref, out_ref, dense, placed):
    for source in range(in_ref.shape[0]):
        dense[source] = in_ref[source].astype(f32)
        rest = dense[source, 200:208]
        rest = jnp.concatenate([rest, pltpu.roll(rest, WIDTH - 16, 1), pltpu.roll(rest, WIDTH - 32, 1)], axis=0)
        for kind in range(2):
            to = slice(10 * source, 10 * source + 10)
            for i in range(10):
                at = 20 * i + 10 * kind
                placed[kind, to, WIDTH * i : WIDTH * i + WIDTH] = dense[source, at : at + 10]
            placed[kind, to, 10 * WIDTH : QUARTER] = rest[10 * kind : 10 * kind + 10, 0:REST]
    out_ref[...] = placed[:, :, 0:QUARTER].astype(bf16)


def place(blocks):
    sources = blocks.shape[0]
    return pl.pallas_call(
        place_kernel,
        out_shape=jax.ShapeDtypeStruct((2, 10 * sources, QUARTER), bf16),
        in_specs=[VMEM_SPEC],
        out_specs=VMEM_SPEC,
        scratch_shapes=[
            pltpu.VMEM((sources, DENSE, WIDTH), f32),
            pltpu.VMEM((2, 10 * sources, 11 * WIDTH), f32),
        ],
        compiler_params=pltpu.CompilerParams(vmem_limit_bytes=8 << 20),
    )(blocks)


def wave_line_of(index, truncation):
    low = jnp.transpose(index[:, 0, 0:10])
    both = jnp.stack([low, truncation - low], axis=1)
    both = both.reshape(TILES, GROUPS, index.shape[0])
    return jnp.transpose(both, (1, 0, 2)).reshape(1, -1)


def on_device(spectral, legendre, wave_pairs, npoints, lat_rows):
    truncation = legendre.shape[1] - 2
    devices = lax.axis_size("wave")
    mine = jnp.concatenate([wave_pairs, lat_rows]).astype(f32)
    mine = jnp.pad(mine, (0, 128 - mine.shape[0]))
    index = lax.all_to_all(jnp.broadcast_to(mine[None, None, :], (devices, 1, 128)), "wave", 0, 0, tiled=True)
    sums = legendre_sums(wave_pairs, spectral, legendre)
    ordered = order_latitudes(index, sums)
    received = lax.all_to_all(ordered, "wave", 0, 0, tiled=True)
    tables = fourier_tables(lat_rows, npoints, index, truncation)
    wave_line = wave_line_of(index, float(truncation))
    blocks = synthesis(lat_rows, npoints, received, wave_line, tables, truncation)
    blocks = lax.all_to_all(blocks, "field", 0, 0, tiled=True)
    return place(blocks)


def solution(mesh):
    placed = (P("wave", None, None, "field"), P("wave", None, None), P("wave"), P(), P("wave"))
    return jax.shard_map(
        on_device,
        mesh=mesh,
        in_specs=placed,
        out_specs=P(None, None, ("wave", "field")),
        check_vma=False,
    )
```

time: 84.9 us -> 76.8 us (0.905)
  the two profiles are of different devices: /device:TPU:6 before, /device:TPU:5 now
where the time goes in v3:
time: 76.8 us; the launch traced here: 76.4 us
  starting transfers between devices  24.6 us (32%)
  blocking collectives  22.5 us (29%)
  Pallas kernels  20.6 us (27%)
  waiting for transfers between devices  6.29 us (8%)
  local copies, waits for them, and re-layouts  1.56 us (2%)
  other arithmetic  0.78 us (1%)
    all_to_all x1, blocking collectives, on_device(): blocks = lax.all_to_all(blocks, 'field', 0, 0, tiled=True)  22.5 us
    all_to_all x1, starting transfers between devices, on_device(): lax.all_to_all(jnp.broadcast_to(mine[None, None, :], (devices, 1, 128)),...  14.3 us
    all_to_all x1, starting transfers between devices, on_device(): received = lax.all_to_all(ordered, 'wave', 0, 0, tiled=True)  10.3 us
    pallas_call x1, Pallas kernels, legendre_sums(): pl.pallas_call(functools.partial(legendre_kernel, rows - 2), out_shape=pl...  7.36 us
    all_to_all x1, waiting for transfers between devices, on_device(): received = lax.all_to_all(ordered, 'wave', 0, 0, tiled=True)  6.29 us
    pallas_call x1, Pallas kernels, synthesis(): pl.pallas_call(functools.partial(synthesis_kernel, float(truncation)), ou...  6.03 us
    pallas_call x1, Pallas kernels, fourier_tables(): pl.pallas_call(functools.partial(table_kernel, float(truncation)), out_sh...  4.93 us
  transfers between devices with their start and end apart: 2, of which 1 were waited for; matrix products, arithmetic and copies ran while one was open for 0% of the time, Pallas kernels for 16%

profile of v3, /device:TPU:5, one launch (start us, length us, event | category | flops | bytes accessed | tf_op | source)
XLA Modules:
  0.0 76.4 jit_solution(6076929055459770262)
XLA Ops:
  0.0 0.7 add_convert_fusion
  0.8 0.6 broadcast_in_dim.2
  1.4 14.3 %all-to-all-start = ((f32[64,1,128]{2,1,0:T(1,128)}), f32[64,1,128]{2,1,0:T(1,128)S(1)}, u32[]{:S(2)}, u32[]{:S(2)}) async-start(f32[64,1,128]{2,1,0:T(1,128)} %broadcast_in_dim.2), calls=%async_computation | async-start | bytes 65536 | tf_op jit(solution)/shard_map/all_to_all | solution.py:342
  15.6 0.0 copy-start.4
  15.7 0.6 copy-done.4
  16.3 0.0 copy-start.2
  16.3 0.0 copy-start.3
  16.3 7.4 %shard_map.73.sums_ref = f32[20,24,256]{2,1,0:T(8,128)S(1)} custom-call(s32[10]{0:T(128)S(1)} %copy-done.4, f32[10,10,2,1281]{3,2,1,0:T(2,128)} %bitcast.12, bf16[10,1281,128]{2,1,0:T(8,128)(2,1)} %leg_ref.1), custom_call_target="tpu_custom_call" | custom-call | tf_op jit(solution)/shard_map/pallas_call | solution.py:59
  23.7 0.0 copy-start
  23.7 0.0 copy-start.1
  23.7 0.0 all-to-all-done.index_ref
  23.7 1.3 %shard_map.74 = bf16[64,16,128]{2,1,0:T(8,128)(2,1)} custom-call(f32[64,1,128]{2,1,0:T(1,128)S(1)} %all-to-all-done.index_ref, f32[20,24,256]{2,1,0:T(8,128)S(1)} %shard_map.73.sums_ref), custom_call_target="tpu_custom_call" | custom-call | tf_op jit(solution)/shard_map/pallas_call | solution.py:94
  25.0 10.3 %all-to-all-start.1 = ((bf16[64,16,128]{2,1,0:T(8,128)(2,1)}), bf16[64,16,128]{2,1,0:T(8,128)(2,1)S(1)}, u32[]{:S(2)}, u32[]{:S(2)}) async-start(bf16[64,16,128]{2,1,0:T(8,128)(2,1)} %shard_map.74), calls=%async_computation.1 | async-start | bytes 524288 | tf_op jit(solution)/shard_map/all_to_all | solution.py:345
  35.3 0.1 copy.10
  35.4 0.1 copy.11
  35.6 0.1 reshape.10.wave_ref
  35.6 0.0 copy-done.2
  35.6 0.0 copy-done.3
  35.7 4.9 %shard_map.75.table_ref = bf16[4,2560,128]{2,1,0:T(8,128)(2,1)S(1)} custom-call(s32[4]{0:T(128)S(1)} %copy-done.3, s32[256]{0:T(256)S(1)} %copy-done.2, f32[64,1,128]{2,1,0:T(1,128)S(1)} %all-to-all-done.index_ref), custom_call_target="tpu_custom_call" | custom-call | tf_op jit(solution)/shard_map/pallas_call | solution.py:156
  40.6 6.3 %all-to-all-done.1.got_ref = bf16[64,16,128]{2,1,0:T(8,128)(2,1)S(1)} async-done(((bf16[64,16,128]{2,1,0:T(8,128)(2,1)}), bf16[64,16,128]{2,1,0:T(8,128)(2,1)S(1)}, u32[]{:S(2)}, u32[]{:S(2)}) %all-to-all-start.1) | async-done | bytes 262176 | tf_op jit(solution)/shard_map/all_to_all | solution.py:345
  46.9 0.0 copy-done
  46.9 0.0 copy-done.1
  46.9 6.0 %shard_map.76 = bf16[8,208,128]{2,1,0:T(8,128)(2,1)S(1)} custom-call(s32[4]{0:T(128)S(1)} %copy-done.3, s32[256]{0:T(256)S(1)} %copy-done.2, bf16[64,16,128]{2,1,0:T(8,128)(2,1)S(1)} %all-to-all-done.1.got_ref, f32[1,1280]{1,0:T(1,128)S(1)} %reshape.10.wave_ref, bf16[240,128]{1,0:T(8,128)(2,1)S(1)} %copy-done, bf16[128,128]{1,0:T(8,128)(2,1)S(1)} %copy-done.1, ...), custom_call_target="tpu_custom_call" | custom-call | tf_op jit(solution)/shard_map/pallas_call | solution.py:285
  52.9 22.5 %all_to_all.15.in_ref = bf16[8,208,128]{2,1,0:T(8,128)(2,1)S(1)} all-to-all(bf16[8,208,128]{2,1,0:T(8,128)(2,1)S(1)} %shard_map.76), channel_id=1, replica_groups=mesh['wave'=64,'field'=8] {'field'}, dimensions={0} | all-to-all | bytes 851968 | tf_op jit(solution)/shard_map/all_to_all | solution.py:349
  75.4 1.0 %shard_map.77 = bf16[2,80,1289]{2,1,0:T(8,128)(2,1)} custom-call(bf16[8,208,128]{2,1,0:T(8,128)(2,1)S(1)} %all_to_all.15.in_ref), custom_call_target="tpu_custom_call" | custom-call | tf_op jit(solution)/shard_map/pallas_call | solution.py:317
  (5 shorter events, 0.1 us)
Async XLA Ops:
  1.4 22.3 %all-to-all-start = ((f32[64,1,128]{2,1,0:T(1,128)}), f32[64,1,128]{2,1,0:T(1,128)S(1)}, u32[]{:S(2)}, u32[]{:S(2)}) async-start(f32[64,1,128]{2,1,0:T(1,128)} %broadcast_in_dim.2), calls=%async_computation | async-start | bytes 65536 | tf_op jit(solution)/shard_map/all_to_all | solution.py:342
  15.6 0.7 copy-start.4
  16.3 19.3 %copy-start.2 = (s32[256]{0:T(256)S(1)}, s32[256]{0:T(256)}, u32[]{:S(2)}) copy-start(s32[256]{0:T(256)} %npoints.3) | copy-start | bytes 3076
  16.3 19.3 %copy-start.3 = (s32[4]{0:T(128)S(1)}, s32[4]{0:T(128)}, u32[]{:S(2)}) copy-start(s32[4]{0:T(128)} %lat_rows.3) | copy-start | bytes 52
  23.7 23.2 %copy-start = (bf16[240,128]{1,0:T(8,128)(2,1)S(1)}, bf16[240,128]{1,0:T(8,128)(2,1)}, u32[]{:S(2)}) copy-start(bf16[240,128]{1,0:T(8,128)(2,1)} %constant.9.clone.select_ref) | copy-start | bytes 184324
  23.7 23.2 %copy-start.1 = (bf16[128,128]{1,0:T(8,128)(2,1)S(1)}, bf16[128,128]{1,0:T(8,128)(2,1)}, u32[]{:S(2)}) copy-start(bf16[128,128]{1,0:T(8,128)(2,1)} %constant.10.clone.reverse_ref) | copy-start | bytes 98308
  25.0 21.9 %all-to-all-start.1 = ((bf16[64,16,128]{2,1,0:T(8,128)(2,1)}), bf16[64,16,128]{2,1,0:T(8,128)(2,1)S(1)}, u32[]{:S(2)}, u32[]{:S(2)}) async-start(bf16[64,16,128]{2,1,0:T(8,128)(2,1)} %shard_map.74), calls=%async_computation.1 | async-start | bytes 524288 | tf_op jit(solution)/shard_map/all_to_all | solution.py:345

commit v4 on v3

--- a/solution.py
+++ b/solution.py
@@ -168,19 +168,21 @@
 
 
 BATCH = 8
-LAST = ROW_PAIR // CHUNK
+BATCHES = 3
 WIDTH = 128
-DENSE = 208
+FIELDS = 10
+DENSE = 104
 REST = QUARTER - 10 * WIDTH
+PART = 16
 
 
 def synthesis_kernel(
-    truncation, lat_rows, npoints, got_ref, wave_ref, select_ref, reverse_ref, table_ref, out_ref, got, parts, left, line, dense
+    truncation, kind, lat_rows, npoints, got_ref, wave_ref, select_ref, reverse_ref, table_ref, out_ref, got, parts, left, line, dense
 ):
     devices = got_ref.shape[0]
     rows = TILES * devices
     depth = GROUPS * rows
-    lane = lax.broadcasted_iota(i32, (ROWS, WIDTH), 1)
+    chunks = BATCH * BATCHES
     got[...] = got_ref[...].reshape(devices * 4 * TILES, WIDTH).astype(f32)
     for l in range(4):
         stacked = jnp.concatenate(
@@ -188,19 +190,22 @@
         ).astype(bf16)
         both = lax.dot_general(select_ref[...], stacked, (((1,), (1,)), ((), ())), preferred_element_type=f32)
         for g in range(GROUPS):
-            k = wave_ref[:, g * rows : (g + 1) * rows]
-            row = lax.broadcasted_iota(i32, (ROWS, rows), 0)
-            scale = jnp.where(row < 10, 1.0, jnp.broadcast_to(k / truncation, (ROWS, rows)))
-            at = 2 * ROWS * g
             for c in range(2):
-                part = both[at + c * ROWS : at + (c + 1) * ROWS] * scale
-                parts[l, c, :, g * rows : (g + 1) * rows] = part.astype(bf16).astype(f32)
+                at = PART * (2 * g + c)
+                part = both[at : at + PART]
+                if kind:
+                    part = part * (wave_ref[:, g * rows : (g + 1) * rows] / truncation)
+                    part = part.astype(bf16).astype(f32)
+                parts[l, c, :, g * rows : (g + 1) * rows] = part
+
+    chunk = lax.broadcasted_iota(i32, (BATCH, rows), 0)
+    place_in = lax.broadcasted_iota(i32, (BATCH, WIDTH), 0) * CHUNK + lax.broadcasted_iota(i32, (BATCH, WIDTH), 1)
+    place_back = lax.broadcasted_iota(i32, (BATCH, WIDTH), 0) * CHUNK - lax.broadcasted_iota(i32, (BATCH, WIDTH), 1)
 
     def batch(l, first, origin):
         n = jnp.full((8, WIDTH), 2 * npoints[lat_rows[l]], i32).astype(f32)
         inverse = (1.0 / n)[0:1, 0:1]
         n = n[0:1, 0:1]
-        chunk = lax.broadcasted_iota(i32, (BATCH, rows), 0)
         center = (2 * CHUNK * (first + chunk) - 2 * origin + CHUNK - 1).astype(f32)
         for g in range(GROUPS):
             at = slice(g * rows, (g + 1) * rows)
@@ -209,122 +214,128 @@
             weight = jnp.where(4.0 * k < n, jnp.where(k == 0.0, 1.0, 2.0), 0.0)
             cosine, sine = sincos(center * k, n, inverse)
             cosine, sine = cosine * weight, sine * weight
-            real, imag = parts[l, 0, :, at], parts[l, 1, :, at]
-            for j in range(0, BATCH, 2):
-                turned = [
-                    (real * cosine[i : i + 1] - imag * sine[i : i + 1], imag * cosine[i : i + 1] + real * sine[i : i + 1])
-                    for i in (j, j + 1)
-                ]
-                to = slice(j * ROWS, (j + 2) * ROWS)
-                left[to, at] = jnp.concatenate([turned[0][0], turned[1][0]], axis=0).astype(bf16)
-                left[to, at_imag] = jnp.concatenate([turned[0][1], turned[1][1]], axis=0).astype(bf16)
+            for f in range(0, FIELDS, 2):
+                turned_real, turned_imag = [], []
+                for i in (f, f + 1):
+                    real, imag = parts[l, 0, i : i + 1, at], parts[l, 1, i : i + 1, at]
+                    turned_real.append(real * cosine - imag * sine)
+                    turned_imag.append(imag * cosine + real * sine)
+                to = slice(f * BATCH, (f + 2) * BATCH)
+                left[to, at] = jnp.concatenate(turned_real, axis=0).astype(bf16)
+                left[to, at_imag] = jnp.concatenate(turned_imag, axis=0).astype(bf16)
         even = jnp.dot(left[:, 0:depth], table_ref[l, 0:depth], preferred_element_type=f32)
         odd = jnp.dot(left[:, depth : 2 * depth], table_ref[l, depth : 2 * depth], preferred_element_type=f32)
         before, after = even + odd, even - odd
-        for j in range(BATCH):
-            tile = 2 * (first + j)
-            at = slice(j * ROWS, (j + 1) * ROWS)
-            line[tile] = jnp.where(WIDTH - 1 - lane + tile * WIDTH >= origin, before[at], line[tile])
-            line[tile + 1] = jnp.where(lane + (tile + 1) * WIDTH >= origin, after[at], line[tile + 1])
-
+        limit = origin - CHUNK * first
+        keep_back = place_back + (WIDTH - 1) >= limit
+        keep_in = place_in + WIDTH >= limit
+        for f in range(FIELDS):
+            at = slice(f * BATCH, (f + 1) * BATCH)
+            to = pl.ds(pl.multiple_of(f * chunks + first, 8), BATCH)
+            line[to] = jnp.where(keep_back, before[at], line[to])
+            to = pl.ds(pl.multiple_of((FIELDS + f) * chunks + first, 8), BATCH)
+            line[to] = jnp.where(keep_in, after[at], line[to])
+
+    lane = lax.broadcasted_iota(i32, (FIELDS, WIDTH), 1)
     for pair in range(2):
         n_a = npoints[lat_rows[2 * pair]]
-        start_b = lax.shift_right_arithmetic(n_a, 8)
-        batches_a = lax.shift_right_arithmetic(lax.shift_right_arithmetic(n_a - 1, 8) + BATCH, 3)
-        batches_b = lax.shift_right_arithmetic(LAST - start_b + BATCH, 3)
+        batches_a = lax.shift_right_arithmetic(n_a - 1, 11) + 1
+        start_b = lax.shift_right_arithmetic(n_a, 11)
 
         def body(step, carry):
             second = step >= batches_a
             l = 2 * pair + jnp.where(second, 1, 0)
-            first = jnp.where(second, start_b + BATCH * (step - batches_a), BATCH * step)
+            first = BATCH * jnp.where(second, step - batches_a + start_b, step)
             batch(l, first, jnp.where(second, n_a, 0))
             return carry
 
-        lax.fori_loop(0, batches_a + batches_b, body, 0)
-        before = jnp.concatenate([line[2 * i] for i in range(LAST + 1)], axis=0).astype(bf16)
-        before = jnp.dot(before, reverse_ref[...], preferred_element_type=f32)
-        for i in range(LAST + 1):
-            line[2 * i] = before[i * ROWS : (i + 1) * ROWS]
+        lax.fori_loop(0, batches_a + BATCHES - start_b, body, 0)
+        back = slice(0, FIELDS * chunks)
+        line[back] = jnp.dot(line[back].astype(bf16), reverse_ref[...], preferred_element_type=f32)
+
+        def tile_of(tile):
+            return line[pl.ds((tile % 2) * FIELDS * chunks + tile // 2, FIELDS, chunks), :]
+
         for q in range(4):
             shift = (QUARTER * q) % WIDTH
             for i in range(QUARTER // WIDTH + 1):
                 tile = QUARTER * q // WIDTH + i
-                v = line[tile]
+                v = tile_of(tile)
                 if shift:
                     v = jnp.where(
                         lane < WIDTH - shift,
                         pltpu.roll(v, WIDTH - shift, 1),
-                        pltpu.roll(line[tile + 1], WIDTH - shift, 1),
+                        pltpu.roll(tile_of(tile + 1), WIDTH - shift, 1),
                     )
                 if i < 10:
-                    dense[q, 20 * i : 20 * i + 20] = v[0:20]
+                    dense[q, FIELDS * i : FIELDS * i + FIELDS] = v
                 else:
-                    spread = lane[0:8]
-                    dense[q, 200:208] = jnp.where(
-                        spread < 16, v[0:8], jnp.where(spread < 32, pltpu.roll(v[8:16], 16, 1), pltpu.roll(v[16:24], 32, 1))
-                    )
+                    dense[q, 100:104] = v[0:4]
+                    dense[q, 100:104, 16:32] = v[4:8, 0:16]
+                    dense[q, 100:102, 32:48] = v[8:10, 0:16]
             out_ref[4 * pair + q] = dense[q].astype(bf16)
 
 
-def select_rows():
-    table = np.zeros((GROUPS, 2 * ROWS, 128), np.float32)
+def select_rows(kind):
+    table = np.zeros((GROUPS, 2, PART, 128), np.float32)
     for g in range(GROUPS):
-        for f in range(10):
+        for f in range(FIELDS):
             real, imag = g * ROWS + 2 * f, g * ROWS + 2 * f + 1
-            table[g, f, real] = 1.0
-            table[g, 10 + f, imag] = -1.0
-            table[g, ROWS + f, imag] = 1.0
-            table[g, ROWS + 10 + f, real] = 1.0
-    return table.reshape(GROUPS * 2 * ROWS, 128).astype(jnp.bfloat16)
-
-
-def synthesis(lat_rows, npoints, received, wave_line, tables, truncation):
+            if kind == 0:
+                table[g, 0, f, real] = 1.0
+                table[g, 1, f, imag] = 1.0
+            else:
+                table[g, 0, f, imag] = -1.0
+                table[g, 1, f, real] = 1.0
+    return table.reshape(GROUPS * 2 * PART, 128).astype(jnp.bfloat16)
+
+
+def synthesis(kind, lat_rows, npoints, received, wave_line, tables, truncation):
     devices = received.shape[0]
     depth = GROUPS * TILES * devices
     reverse = np.eye(WIDTH)[::-1].astype(jnp.bfloat16)
     return pl.pallas_call(
-        functools.partial(synthesis_kernel, float(truncation)),
+        functools.partial(synthesis_kernel, float(truncation), kind),
         out_shape=jax.ShapeDtypeStruct((8, DENSE, WIDTH), bf16),
         in_specs=[pl.BlockSpec(memory_space=pltpu.SMEM)] * 2 + [VMEM_SPEC] * 5,
         out_specs=VMEM_SPEC,
         scratch_shapes=[
             pltpu.VMEM((devices * 4 * TILES, WIDTH), f32),
-            pltpu.VMEM((4, 2, ROWS, depth), f32),
-            pltpu.VMEM((BATCH * ROWS, 2 * depth), bf16),
-            pltpu.VMEM((2 * (LAST + BATCH) + 2, ROWS, WIDTH), f32),
+            pltpu.VMEM((4, 2, PART, depth), f32),
+            pltpu.VMEM((BATCH * FIELDS, 2 * depth), bf16),
+            pltpu.VMEM((2 * FIELDS * BATCH * BATCHES, WIDTH), f32),
             pltpu.VMEM((4, DENSE, WIDTH), f32),
         ],
         compiler_params=pltpu.CompilerParams(vmem_limit_bytes=16 << 20),
-    )(lat_rows, npoints, received, wave_line, select_rows(), reverse, tables)
-
-
-def place_kernel(in_ref, out_ref, dense, placed):
-    for source in range(in_ref.shape[0]):
-        dense[source] = in_ref[source].astype(f32)
-        rest = dense[source, 200:208]
-        rest = jnp.concatenate([rest, pltpu.roll(rest, WIDTH - 16, 1), pltpu.roll(rest, WIDTH - 32, 1)], axis=0)
-        for kind in range(2):
-            to = slice(10 * source, 10 * source + 10)
+    )(lat_rows, npoints, received, wave_line, select_rows(kind), reverse, tables)
+
+
+def place_kernel(value_ref, slope_ref, out_ref, dense, placed):
+    for source in range(value_ref.shape[0]):
+        for kind, in_ref in enumerate((value_ref, slope_ref)):
+            dense[source] = in_ref[source].astype(f32)
+            to = slice(FIELDS * source, FIELDS * source + FIELDS)
             for i in range(10):
-                at = 20 * i + 10 * kind
-                placed[kind, to, WIDTH * i : WIDTH * i + WIDTH] = dense[source, at : at + 10]
-            placed[kind, to, 10 * WIDTH : QUARTER] = rest[10 * kind : 10 * kind + 10, 0:REST]
+                placed[kind, to, WIDTH * i : WIDTH * i + WIDTH] = dense[source, FIELDS * i : FIELDS * i + FIELDS]
+            rest = dense[source, 100:104]
+            rest = jnp.concatenate([rest[:, 0:16], rest[:, 16:32], rest[0:2, 32:48]], axis=0)
+            placed[kind, to, 10 * WIDTH : QUARTER] = rest[:, 0:REST]
     out_ref[...] = placed[:, :, 0:QUARTER].astype(bf16)
 
 
-def place(blocks):
-    sources = blocks.shape[0]
+def place(values, slopes):
+    sources = values.shape[0]
     return pl.pallas_call(
         place_kernel,
-        out_shape=jax.ShapeDtypeStruct((2, 10 * sources, QUARTER), bf16),
-        in_specs=[VMEM_SPEC],
+        out_shape=jax.ShapeDtypeStruct((2, FIELDS * sources, QUARTER), bf16),
+        in_specs=[VMEM_SPEC] * 2,
         out_specs=VMEM_SPEC,
         scratch_shapes=[
             pltpu.VMEM((sources, DENSE, WIDTH), f32),
-            pltpu.VMEM((2, 10 * sources, 11 * WIDTH), f32),
+            pltpu.VMEM((2, FIELDS * sources, 11 * WIDTH), f32),
         ],
         compiler_params=pltpu.CompilerParams(vmem_limit_bytes=8 << 20),
-    )(blocks)
+    )(values, slopes)
 
 
 def wave_line_of(index, truncation):
@@ -345,9 +356,11 @@
     received = lax.all_to_all(ordered, "wave", 0, 0, tiled=True)
     tables = fourier_tables(lat_rows, npoints, index, truncation)
     wave_line = wave_line_of(index, float(truncation))
-    blocks = synthesis(lat_rows, npoints, received, wave_line, tables, truncation)
-    blocks = lax.all_to_all(blocks, "field", 0, 0, tiled=True)
-    return place(blocks)
+    blocks = []
+    for kind in range(2):
+        block = synthesis(kind, lat_rows, npoints, received, wave_line, tables, truncation)
+        blocks.append(lax.all_to_all(block, "field", 0, 0, tiled=True))
+    return place(*blocks)
 
 
 def solution(mesh):

time: 76.8 us -> 83.9 us (1.092)
  the two profiles are of different devices: /device:TPU:5 before, /device:TPU:6 now
where the time goes in v4:
time: 83.9 us; the launch traced here: 83.4 us
  starting transfers between devices  31.4 us (37%)
  Pallas kernels  24.2 us (29%)
  waiting for transfers between devices  12.9 us (15%)
  blocking collectives  12.4 us (15%)
  local copies, waits for them, and re-layouts  1.57 us (2%)
    all_to_all x1, starting transfers between devices, on_device(): lax.all_to_all(jnp.broadcast_to(mine[None, None, :], (devices, 1, 128)),...  14 us
    all_to_all x1, blocking collectives, on_device(): blocks.append(lax.all_to_all(block, 'field', 0, 0, tiled=True))  12.4 us
    all_to_all x1, starting transfers between devices, on_device(): received = lax.all_to_all(ordered, 'wave', 0, 0, tiled=True)  10.3 us
    pallas_call x2, Pallas kernels, synthesis(): pl.pallas_call(functools.partial(synthesis_kernel, float(truncation), kin...  9.62 us
    pallas_call x1, Pallas kernels, legendre_sums(): pl.pallas_call(functools.partial(legendre_kernel, rows - 2), out_shape=pl...  7.36 us
    all_to_all x1, starting transfers between devices, on_device(): blocks.append(lax.all_to_all(block, 'field', 0, 0, tiled=True))  7.11 us
    all_to_all x1, waiting for transfers between devices, on_device(): blocks.append(lax.all_to_all(block, 'field', 0, 0, tiled=True))  6.64 us
    all_to_all x1, waiting for transfers between devices, on_device(): received = lax.all_to_all(ordered, 'wave', 0, 0, tiled=True)  6.29 us
  transfers between devices with their start and end apart: 3, of which 2 were waited for; matrix products, arithmetic and copies ran while one was open for 0% of the time, Pallas kernels for 20%

profile of v4, /device:TPU:6, one launch (start us, length us, event | category | flops | bytes accessed | tf_op | source)
XLA Modules:
  0.0 83.4 jit_solution(5441521677268895622)
XLA Ops:
  0.0 0.7 add_convert_fusion
  0.8 0.6 broadcast_in_dim.2
  1.4 14.0 %all-to-all-start = ((f32[64,1,128]{2,1,0:T(1,128)}), f32[64,1,128]{2,1,0:T(1,128)S(1)}, u32[]{:S(2)}, u32[]{:S(2)}) async-start(f32[64,1,128]{2,1,0:T(1,128)} %broadcast_in_dim.2), calls=%async_computation | async-start | bytes 65536 | tf_op jit(solution)/shard_map/all_to_all | solution.py:353
  15.4 0.0 copy-start.5
  15.4 0.6 copy-done.5
  16.1 0.0 copy-start.3
  16.1 0.0 copy-start.4
  16.1 7.4 %shard_map.91.sums_ref = f32[20,24,256]{2,1,0:T(8,128)S(1)} custom-call(s32[10]{0:T(128)S(1)} %copy-done.5, f32[10,10,2,1281]{3,2,1,0:T(2,128)} %bitcast.12, bf16[10,1281,128]{2,1,0:T(8,128)(2,1)} %leg_ref.1), custom_call_target="tpu_custom_call" | custom-call | tf_op jit(solution)/shard_map/pallas_call | solution.py:59
  23.4 0.0 copy-start
  23.5 0.0 copy-start.2
  23.5 0.0 all-to-all-done.index_ref
  23.5 1.3 %shard_map.92 = bf16[64,16,128]{2,1,0:T(8,128)(2,1)} custom-call(f32[64,1,128]{2,1,0:T(1,128)S(1)} %all-to-all-done.index_ref, f32[20,24,256]{2,1,0:T(8,128)S(1)} %shard_map.91.sums_ref), custom_call_target="tpu_custom_call" | custom-call | tf_op jit(solution)/shard_map/pallas_call | solution.py:94
  24.8 10.3 %all-to-all-start.1 = ((bf16[64,16,128]{2,1,0:T(8,128)(2,1)}), bf16[64,16,128]{2,1,0:T(8,128)(2,1)S(1)}, u32[]{:S(2)}, u32[]{:S(2)}) async-start(bf16[64,16,128]{2,1,0:T(8,128)(2,1)} %shard_map.92), calls=%async_computation.1 | async-start | bytes 524288 | tf_op jit(solution)/shard_map/all_to_all | solution.py:356
  35.1 0.1 copy.12
  35.2 0.1 copy.13
  35.3 0.1 reshape.10.wave_ref
  35.4 0.0 copy-done.3
  35.4 0.0 copy-done.4
  35.4 0.0 copy-start.1
  35.4 4.9 %shard_map.93.table_ref = bf16[4,2560,128]{2,1,0:T(8,128)(2,1)S(1)} custom-call(s32[4]{0:T(128)S(1)} %copy-done.4, s32[256]{0:T(256)S(1)} %copy-done.3, f32[64,1,128]{2,1,0:T(1,128)S(1)} %all-to-all-done.index_ref), custom_call_target="tpu_custom_call" | custom-call | tf_op jit(solution)/shard_map/pallas_call | solution.py:156
  40.4 6.3 %all-to-all-done.1.got_ref = bf16[64,16,128]{2,1,0:T(8,128)(2,1)S(1)} async-done(((bf16[64,16,128]{2,1,0:T(8,128)(2,1)}), bf16[64,16,128]{2,1,0:T(8,128)(2,1)S(1)}, u32[]{:S(2)}, u32[]{:S(2)}) %all-to-all-start.1) | async-done | bytes 262176 | tf_op jit(solution)/shard_map/all_to_all | solution.py:356
  46.7 0.0 copy-done
  46.7 0.0 copy-done.2
  46.7 5.2 %shard_map.94 = bf16[8,104,128]{2,1,0:T(8,128)(2,1)} custom-call(s32[4]{0:T(128)S(1)} %copy-done.4, s32[256]{0:T(256)S(1)} %copy-done.3, bf16[64,16,128]{2,1,0:T(8,128)(2,1)S(1)} %all-to-all-done.1.got_ref, f32[1,1280]{1,0:T(1,128)S(1)} %reshape.10.wave_ref, bf16[160,128]{1,0:T(8,128)(2,1)S(1)} %copy-done.2, bf16[128,128]{1,0:T(8,128)(2,1)S(1)} %copy-done, ...), custom_call_target="tpu_custom_call" | custom-call | tf_op jit(solution)/shard_map/pallas_call | solution.py:297
  51.8 7.1 %all-to-all-start.2 = ((bf16[8,104,128]{2,1,0:T(8,128)(2,1)}), bf16[8,104,128]{2,1,0:T(8,128)(2,1)S(1)}, u32[]{:S(2)}, u32[]{:S(2)}) async-start(bf16[8,104,128]{2,1,0:T(8,128)(2,1)} %shard_map.94), calls=%async_computation.2 | async-start | bytes 425984 | tf_op jit(solution)/shard_map/all_to_all | solution.py:362
  58.9 0.0 copy-done.1
  58.9 4.5 %shard_map.95 = bf16[8,104,128]{2,1,0:T(8,128)(2,1)S(1)} custom-call(s32[4]{0:T(128)S(1)} %copy-done.4, s32[256]{0:T(256)S(1)} %copy-done.3, bf16[64,16,128]{2,1,0:T(8,128)(2,1)S(1)} %all-to-all-done.1.got_ref, f32[1,1280]{1,0:T(1,128)S(1)} %reshape.10.wave_ref, bf16[160,128]{1,0:T(8,128)(2,1)S(1)} %copy-done.1, bf16[128,128]{1,0:T(8,128)(2,1)S(1)} %copy-done, ...), custom_call_target="tpu_custom_call" | custom-call | tf_op jit(solution)/shard_map/pallas_call | solution.py:297
  63.4 6.6 %all-to-all-done.2.value_ref = bf16[8,104,128]{2,1,0:T(8,128)(2,1)S(1)} async-done(((bf16[8,104,128]{2,1,0:T(8,128)(2,1)}), bf16[8,104,128]{2,1,0:T(8,128)(2,1)S(1)}, u32[]{:S(2)}, u32[]{:S(2)}) %all-to-all-start.2) | async-done | bytes 213024 | tf_op jit(solution)/shard_map/all_to_all | solution.py:362
  70.0 12.4 %all_to_all.20.slope_ref = bf16[8,104,128]{2,1,0:T(8,128)(2,1)S(1)} all-to-all(bf16[8,104,128]{2,1,0:T(8,128)(2,1)S(1)} %shard_map.95), channel_id=1, replica_groups=mesh['wave'=64,'field'=8] {'field'}, dimensions={0} | all-to-all | bytes 425984 | tf_op jit(solution)/shard_map/all_to_all | solution.py:362
  82.4 1.0 %shard_map.96 = bf16[2,80,1289]{2,1,0:T(8,128)(2,1)} custom-call(bf16[8,104,128]{2,1,0:T(8,128)(2,1)S(1)} %all-to-all-done.2.value_ref, bf16[8,104,128]{2,1,0:T(8,128)(2,1)S(1)} %all_to_all.20.slope_ref), custom_call_target="tpu_custom_call" | custom-call | tf_op jit(solution)/shard_map/pallas_call | solution.py:328
  (5 shorter events, 0.1 us)
Async XLA Ops:
  1.4 22.1 %all-to-all-start = ((f32[64,1,128]{2,1,0:T(1,128)}), f32[64,1,128]{2,1,0:T(1,128)S(1)}, u32[]{:S(2)}, u32[]{:S(2)}) async-start(f32[64,1,128]{2,1,0:T(1,128)} %broadcast_in_dim.2), calls=%async_computation | async-start | bytes 65536 | tf_op jit(solution)/shard_map/all_to_all | solution.py:353
  15.4 0.7 copy-start.5
  16.1 19.3 %copy-start.3 = (s32[256]{0:T(256)S(1)}, s32[256]{0:T(256)}, u32[]{:S(2)}) copy-start(s32[256]{0:T(256)} %npoints.5) | copy-start | bytes 3076
  16.1 19.3 %copy-start.4 = (s32[4]{0:T(128)S(1)}, s32[4]{0:T(128)}, u32[]{:S(2)}) copy-start(s32[4]{0:T(128)} %lat_rows.5) | copy-start | bytes 52
  23.4 23.2 %copy-start = (bf16[128,128]{1,0:T(8,128)(2,1)S(1)}, bf16[128,128]{1,0:T(8,128)(2,1)}, u32[]{:S(2)}) copy-start(bf16[128,128]{1,0:T(8,128)(2,1)} %constant.12.clone.reverse_ref) | copy-start | bytes 98308
  23.5 23.2 %copy-start.2 = (bf16[160,128]{1,0:T(8,128)(2,1)S(1)}, bf16[160,128]{1,0:T(8,128)(2,1)}, u32[]{:S(2)}) copy-start(bf16[160,128]{1,0:T(8,128)(2,1)} %constant.11.clone.select_ref) | copy-start | bytes 122884
  24.8 21.9 %all-to-all-start.1 = ((bf16[64,16,128]{2,1,0:T(8,128)(2,1)}), bf16[64,16,128]{2,1,0:T(8,128)(2,1)S(1)}, u32[]{:S(2)}, u32[]{:S(2)}) async-start(bf16[64,16,128]{2,1,0:T(8,128)(2,1)} %shard_map.92), calls=%async_computation.1 | async-start | bytes 524288 | tf_op jit(solution)/shard_map/all_to_all | solution.py:356
  35.4 23.5 %copy-start.1 = (bf16[160,128]{1,0:T(8,128)(2,1)S(1)}, bf16[160,128]{1,0:T(8,128)(2,1)}, u32[]{:S(2)}) copy-start(bf16[160,128]{1,0:T(8,128)(2,1)} %constant.13.clone.select_ref) | copy-start | bytes 122884
  51.8 18.2 %all-to-all-start.2 = ((bf16[8,104,128]{2,1,0:T(8,128)(2,1)}), bf16[8,104,128]{2,1,0:T(8,128)(2,1)S(1)}, u32[]{:S(2)}, u32[]{:S(2)}) async-start(bf16[8,104,128]{2,1,0:T(8,128)(2,1)} %shard_map.94), calls=%async_computation.2 | async-start | bytes 425984 | tf_op jit(solution)/shard_map/all_to_all | solution.py:362

commit v5 on v3

--- a/solution.py
+++ b/solution.py
@@ -20,35 +20,47 @@
 VMEM_SPEC = pl.BlockSpec(memory_space=pltpu.VMEM)
 
 
-def legendre_kernel(truncation, waves, spec_ref, leg_ref, out_ref, coeffs):
-    slot = pl.program_id(0)
+def legendre_kernel(truncation, waves, spec_hbm, leg_hbm, out_ref, spec_ref, leg_ref, coeffs, spec_sems, leg_sems):
     rows = truncation + 2
-    fields = spec_ref.shape[1]
-
-    @pl.when(slot == 0)
-    def _():
-        coeffs[...] = jnp.zeros_like(coeffs)
-
-    for field in range(fields):
-        coeffs[2 * field : 2 * field + 2, 0:rows] = spec_ref[0, field]
-    split = truncation + 1 - waves[slot]
-    row = lax.broadcasted_iota(i32, (1, rows), 1)
-    low = row < split
-    offset = jnp.where(low, row, row - split)
-    sign = jnp.where(offset % 2 == 0, 1.0, -1.0).astype(f32)
-    low = jnp.where(low, 1.0, 0.0).astype(f32)
-    high = 1.0 - low
-    values = coeffs[:, 0:rows]
-    stacked = jnp.concatenate([values * mask for mask in (low, low * sign, high, high * sign)], axis=0)
-    stacked = stacked.astype(bf16)
+    slots, fields = spec_ref.shape[0], spec_ref.shape[1]
     main = rows - 1
-    sums = jnp.dot(stacked[:, 0:main], leg_ref[0, 0:main, :], preferred_element_type=f32)
-    last = stacked[:, main:rows].astype(f32) * leg_ref[0, main:rows, :].astype(f32)
-    sums = sums + last
-    for half in range(2):
-        for side in range(2):
-            at = (2 * half + side) * ROWS
-            out_ref[half, :, 128 * side : 128 * side + 128] = sums[at : at + ROWS, :]
+
+    def copies(slot):
+        return (
+            pltpu.make_async_copy(spec_hbm.at[slot], spec_ref.at[slot], spec_sems.at[slot]),
+            pltpu.make_async_copy(leg_hbm.at[slot], leg_ref.at[slot], leg_sems.at[slot]),
+        )
+
+    for slot in range(slots):
+        for copy in copies(slot):
+            copy.start()
+    coeffs[...] = jnp.zeros_like(coeffs)
+
+    def body(slot, carry):
+        for copy in copies(slot):
+            copy.wait()
+        for field in range(fields):
+            coeffs[2 * field : 2 * field + 2, 0:rows] = spec_ref[slot, field]
+        split = truncation + 1 - waves[slot]
+        row = lax.broadcasted_iota(i32, (1, rows), 1)
+        low = row < split
+        offset = jnp.where(low, row, row - split)
+        sign = jnp.where(offset % 2 == 0, 1.0, -1.0).astype(f32)
+        low = jnp.where(low, 1.0, 0.0).astype(f32)
+        high = 1.0 - low
+        values = coeffs[:, 0:rows]
+        stacked = jnp.concatenate([values * mask for mask in (low, low * sign, high, high * sign)], axis=0)
+        stacked = stacked.astype(bf16)
+        sums = jnp.dot(stacked[:, 0:main], leg_ref[slot, 0:main, :], preferred_element_type=f32)
+        last = stacked[:, main:rows].astype(f32) * leg_ref[slot, main:rows, :].astype(f32)
+        sums = sums + last
+        for half in range(2):
+            for side in range(2):
+                at = (2 * half + side) * ROWS
+                out_ref[2 * slot + half, :, 128 * side : 128 * side + 128] = sums[at : at + ROWS, :]
+        return carry
+
+    lax.fori_loop(0, slots, body, 0)
 
 
 def legendre_sums(wave_pairs, spectral, legendre):
@@ -59,18 +71,35 @@
     return pl.pallas_call(
         functools.partial(legendre_kernel, rows - 2),
         out_shape=pltpu.VMEM((2 * slots, ROWS, 2 * northern), f32),
-        grid_spec=pltpu.PrefetchScalarGridSpec(
-            num_scalar_prefetch=1,
-            grid=(slots,),
-            in_specs=[
-                pl.BlockSpec((1, fields, 2, rows), lambda p, w: (p, 0, 0, 0)),
-                pl.BlockSpec((1, rows, northern), lambda p, w: (p, 0, 0)),
-            ],
-            out_specs=pl.BlockSpec((2, ROWS, 2 * northern), lambda p, w: (p, 0, 0)),
-            scratch_shapes=[pltpu.VMEM((ROWS, 1408), f32)],
-        ),
-        compiler_params=pltpu.CompilerParams(vmem_limit_bytes=8 << 20),
-    )(wave_pairs, parts, legendre)
+        in_specs=[pl.BlockSpec(memory_space=pltpu.SMEM)] + [pl.BlockSpec(memory_space=pltpu.HBM)] * 2,
+        out_specs=VMEM_SPEC,
+        scratch_shapes=[
+            pltpu.VMEM((slots, fields, 2, rows), f32),
+            pltpu.VMEM((slots, rows, northern), bf16),
+            pltpu.VMEM((ROWS, 1408), f32),
+            pltpu.SemaphoreType.DMA((slots,)),
+            pltpu.SemaphoreType.DMA((slots,)),
+        ],
+        compiler_params=pltpu.CompilerParams(vmem_limit_bytes=16 << 20),
+    )(pltpu.with_memory_space_constraint(wave_pairs, pltpu.HBM), parts, legendre)
+
+
+def announce_kernel(waves, lats, out_ref):
+    lane = lax.broadcasted_iota(i32, (1, 128), 1)
+    row = jnp.zeros((1, 128), i32)
+    for i in range(14):
+        row = jnp.where(lane == i, waves[i] if i < 10 else lats[i - 10], row)
+    out_ref[...] = jnp.broadcast_to(row.astype(f32).reshape(1, 1, 128), out_ref.shape)
+
+
+def announcement(wave_pairs, lat_rows, devices):
+    return pl.pallas_call(
+        announce_kernel,
+        out_shape=jax.ShapeDtypeStruct((devices, 1, 128), f32),
+        in_specs=[pl.BlockSpec(memory_space=pltpu.SMEM)] * 2,
+        out_specs=VMEM_SPEC,
+        compiler_params=pltpu.CompilerParams(vmem_limit_bytes=1 << 20),
+    )(*(pltpu.with_memory_space_constraint(x, pltpu.HBM) for x in (wave_pairs, lat_rows)))
 
 
 def order_kernel(index_ref, sums_ref, out_ref, scratch):
@@ -168,8 +197,9 @@
 
 
 BATCH = 8
-LAST = ROW_PAIR // CHUNK
+BATCHES = 3
 WIDTH = 128
+COLUMNS = 20
 DENSE = 208
 REST = QUARTER - 10 * WIDTH
 
@@ -180,7 +210,7 @@
     devices = got_ref.shape[0]
     rows = TILES * devices
     depth = GROUPS * rows
-    lane = lax.broadcasted_iota(i32, (ROWS, WIDTH), 1)
+    chunks = BATCH * BATCHES
     got[...] = got_ref[...].reshape(devices * 4 * TILES, WIDTH).astype(f32)
     for l in range(4):
         stacked = jnp.concatenate(
@@ -188,81 +218,89 @@
         ).astype(bf16)
         both = lax.dot_general(select_ref[...], stacked, (((1,), (1,)), ((), ())), preferred_element_type=f32)
         for g in range(GROUPS):
-            k = wave_ref[:, g * rows : (g + 1) * rows]
+            at = slice(g * rows, (g + 1) * rows)
             row = lax.broadcasted_iota(i32, (ROWS, rows), 0)
-            scale = jnp.where(row < 10, 1.0, jnp.broadcast_to(k / truncation, (ROWS, rows)))
-            at = 2 * ROWS * g
+            scale = jnp.where(row < 10, 1.0, jnp.broadcast_to(wave_ref[:, at] / truncation, (ROWS, rows)))
             for c in range(2):
-                part = both[at + c * ROWS : at + (c + 1) * ROWS] * scale
-                parts[l, c, :, g * rows : (g + 1) * rows] = part.astype(bf16).astype(f32)
+                part = both[ROWS * (2 * g + c) : ROWS * (2 * g + c + 1)] * scale
+                parts[l, c, :, at] = part.astype(bf16).astype(f32)
+
+    chunk = lax.broadcasted_iota(i32, (BATCH, depth), 0)
+    place_in = lax.broadcasted_iota(i32, (BATCH, WIDTH), 0) * CHUNK + lax.broadcasted_iota(i32, (BATCH, WIDTH), 1)
+    place_back = lax.broadcasted_iota(i32, (BATCH, WIDTH), 0) * CHUNK - lax.broadcasted_iota(i32, (BATCH, WIDTH), 1)
 
     def batch(l, first, origin):
         n = jnp.full((8, WIDTH), 2 * npoints[lat_rows[l]], i32).astype(f32)
         inverse = (1.0 / n)[0:1, 0:1]
         n = n[0:1, 0:1]
-        chunk = lax.broadcasted_iota(i32, (BATCH, rows), 0)
         center = (2 * CHUNK * (first + chunk) - 2 * origin + CHUNK - 1).astype(f32)
+        k = wave_ref[...]
+        weight = jnp.where(4.0 * k < n, jnp.where(k == 0.0, 1.0, 2.0), 0.0)
+        all_cosine, all_sine = sincos(center * k, n, inverse)
+        all_cosine, all_sine = all_cosine * weight, all_sine * weight
         for g in range(GROUPS):
             at = slice(g * rows, (g + 1) * rows)
             at_imag = slice(depth + g * rows, depth + (g + 1) * rows)
-            k = wave_ref[:, at]
-            weight = jnp.where(4.0 * k < n, jnp.where(k == 0.0, 1.0, 2.0), 0.0)
-            cosine, sine = sincos(center * k, n, inverse)
-            cosine, sine = cosine * weight, sine * weight
-            real, imag = parts[l, 0, :, at], parts[l, 1, :, at]
-            for j in range(0, BATCH, 2):
-                turned = [
-                    (real * cosine[i : i + 1] - imag * sine[i : i + 1], imag * cosine[i : i + 1] + real * sine[i : i + 1])
-                    for i in (j, j + 1)
-                ]
-                to = slice(j * ROWS, (j + 2) * ROWS)
-                left[to, at] = jnp.concatenate([turned[0][0], turned[1][0]], axis=0).astype(bf16)
-                left[to, at_imag] = jnp.concatenate([turned[0][1], turned[1][1]], axis=0).astype(bf16)
+            cosine, sine = all_cosine[:, at], all_sine[:, at]
+            for f in range(0, COLUMNS, 2):
+                turned_real, turned_imag = [], []
+                for i in (f, f + 1):
+                    real, imag = parts[l, 0, i : i + 1, at], parts[l, 1, i : i + 1, at]
+                    turned_real.append(real * cosine - imag * sine)
+                    turned_imag.append(imag * cosine + real * sine)
+                to = slice(f * BATCH, (f + 2) * BATCH)
+                left[to, at] = jnp.concatenate(turned_real, axis=0).astype(bf16)
+                left[to, at_imag] = jnp.concatenate(turned_imag, axis=0).astype(bf16)
         even = jnp.dot(left[:, 0:depth], table_ref[l, 0:depth], preferred_element_type=f32)
         odd = jnp.dot(left[:, depth : 2 * depth], table_ref[l, depth : 2 * depth], preferred_element_type=f32)
         before, after = even + odd, even - odd
-        for j in range(BATCH):
-            tile = 2 * (first + j)
-            at = slice(j * ROWS, (j + 1) * ROWS)
-            line[tile] = jnp.where(WIDTH - 1 - lane + tile * WIDTH >= origin, before[at], line[tile])
-            line[tile + 1] = jnp.where(lane + (tile + 1) * WIDTH >= origin, after[at], line[tile + 1])
-
+        limit = origin - CHUNK * first
+        keep_back = place_back + (WIDTH - 1) >= limit
+        keep_in = place_in + WIDTH >= limit
+        for f in range(COLUMNS):
+            at = slice(f * BATCH, (f + 1) * BATCH)
+            to = pl.ds(pl.multiple_of(f * chunks + first, 8), BATCH)
+            line[to] = jnp.where(keep_back, before[at], line[to])
+            to = pl.ds(pl.multiple_of((COLUMNS + f) * chunks + first, 8), BATCH)
+            line[to] = jnp.where(keep_in, after[at], line[to])
+
+    lane = lax.broadcasted_iota(i32, (COLUMNS, WIDTH), 1)
     for pair in range(2):
         n_a = npoints[lat_rows[2 * pair]]
-        start_b = lax.shift_right_arithmetic(n_a, 8)
-        batches_a = lax.shift_right_arithmetic(lax.shift_right_arithmetic(n_a - 1, 8) + BATCH, 3)
-        batches_b = lax.shift_right_arithmetic(LAST - start_b + BATCH, 3)
+        batches_a = lax.shift_right_arithmetic(n_a - 1, 11) + 1
+        start_b = lax.shift_right_arithmetic(n_a, 11)
 
         def body(step, carry):
             second = step >= batches_a
             l = 2 * pair + jnp.where(second, 1, 0)
-            first = jnp.where(second, start_b + BATCH * (step - batches_a), BATCH * step)
+            first = BATCH * jnp.where(second, step - batches_a + start_b, step)
             batch(l, first, jnp.where(second, n_a, 0))
             return carry
 
-        lax.fori_loop(0, batches_a + batches_b, body, 0)
-        before = jnp.concatenate([line[2 * i] for i in range(LAST + 1)], axis=0).astype(bf16)
-        before = jnp.dot(before, reverse_ref[...], preferred_element_type=f32)
-        for i in range(LAST + 1):
-            line[2 * i] = before[i * ROWS : (i + 1) * ROWS]
+        lax.fori_loop(0, batches_a + BATCHES - start_b, body, 0)
+        back = slice(0, COLUMNS * chunks)
+        line[back] = jnp.dot(line[back].astype(bf16), reverse_ref[...], preferred_element_type=f32)
+
+        def tile_of(tile):
+            return line[pl.ds((tile % 2) * COLUMNS * chunks + tile // 2, COLUMNS, chunks), :]
+
         for q in range(4):
             shift = (QUARTER * q) % WIDTH
             for i in range(QUARTER // WIDTH + 1):
                 tile = QUARTER * q // WIDTH + i
-                v = line[tile]
+                v = tile_of(tile)
                 if shift:
                     v = jnp.where(
                         lane < WIDTH - shift,
                         pltpu.roll(v, WIDTH - shift, 1),
-                        pltpu.roll(line[tile + 1], WIDTH - shift, 1),
+                        pltpu.roll(tile_of(tile + 1), WIDTH - shift, 1),
                     )
                 if i < 10:
-                    dense[q, 20 * i : 20 * i + 20] = v[0:20]
+                    dense[q, COLUMNS * i : COLUMNS * i + COLUMNS] = v
                 else:
-                    spread = lane[0:8]
-                    dense[q, 200:208] = jnp.where(
-                        spread < 16, v[0:8], jnp.where(spread < 32, pltpu.roll(v[8:16], 16, 1), pltpu.roll(v[16:24], 32, 1))
-                    )
+                    dense[q, 200:208] = v[0:8]
+                    dense[q, 200:208, 16:32] = v[8:16, 0:16]
+                    dense[q, 200:204, 32:48] = v[16:20, 0:16]
             out_ref[4 * pair + q] = dense[q].astype(bf16)
 
 
@@ -290,8 +328,8 @@
         scratch_shapes=[
             pltpu.VMEM((devices * 4 * TILES, WIDTH), f32),
             pltpu.VMEM((4, 2, ROWS, depth), f32),
-            pltpu.VMEM((BATCH * ROWS, 2 * depth), bf16),
-            pltpu.VMEM((2 * (LAST + BATCH) + 2, ROWS, WIDTH), f32),
+            pltpu.VMEM((BATCH * COLUMNS, 2 * depth), bf16),
+            pltpu.VMEM((2 * COLUMNS * BATCH * BATCHES, WIDTH), f32),
             pltpu.VMEM((4, DENSE, WIDTH), f32),
         ],
         compiler_params=pltpu.CompilerParams(vmem_limit_bytes=16 << 20),
@@ -337,17 +375,14 @@
 def on_device(spectral, legendre, wave_pairs, npoints, lat_rows):
     truncation = legendre.shape[1] - 2
     devices = lax.axis_size("wave")
-    mine = jnp.concatenate([wave_pairs, lat_rows]).astype(f32)
-    mine = jnp.pad(mine, (0, 128 - mine.shape[0]))
-    index = lax.all_to_all(jnp.broadcast_to(mine[None, None, :], (devices, 1, 128)), "wave", 0, 0, tiled=True)
+    index = lax.all_to_all(announcement(wave_pairs, lat_rows, devices), "wave", 0, 0, tiled=True)
     sums = legendre_sums(wave_pairs, spectral, legendre)
     ordered = order_latitudes(index, sums)
     received = lax.all_to_all(ordered, "wave", 0, 0, tiled=True)
     tables = fourier_tables(lat_rows, npoints, index, truncation)
     wave_line = wave_line_of(index, float(truncation))
     blocks = synthesis(lat_rows, npoints, received, wave_line, tables, truncation)
-    blocks = lax.all_to_all(blocks, "field", 0, 0, tiled=True)
-    return place(blocks)
+    return place(lax.all_to_all(blocks, "field", 0, 0, tiled=True))
 
 
 def solution(mesh):

time: 76.8 us -> 72.3 us (0.941)
  the two profiles are of different devices: /device:TPU:5 before, /device:TPU:6 now
where the time goes in v5:
time: 72.3 us; the launch traced here: 72 us
  blocking collectives  22.6 us (31%)
  starting transfers between devices  21.4 us (30%)
  Pallas kernels  18.4 us (25%)
  waiting for transfers between devices  9.29 us (13%)
    all_to_all x1, blocking collectives, on_device(): return place(lax.all_to_all(blocks, 'field', 0, 0, tiled=True))  22.6 us
    all_to_all x1, starting transfers between devices, on_device(): lax.all_to_all(announcement(wave_pairs, lat_rows, devices), 'wave', 0, 0,...  14 us
    all_to_all x1, starting transfers between devices, on_device(): received = lax.all_to_all(ordered, 'wave', 0, 0, tiled=True)  7.35 us
    all_to_all x1, waiting for transfers between devices, on_device(): received = lax.all_to_all(ordered, 'wave', 0, 0, tiled=True)  6.31 us
    pallas_call x1, Pallas kernels, synthesis(): pl.pallas_call(functools.partial(synthesis_kernel, float(truncation)), ou...  5.42 us
    pallas_call x1, Pallas kernels, fourier_tables(): pl.pallas_call(functools.partial(table_kernel, float(truncation)), out_sh...  4.93 us
    pallas_call x1, Pallas kernels, legendre_sums(): pl.pallas_call(functools.partial(legendre_kernel, rows - 2), out_shape=pl...  4.46 us
    all_to_all x1, waiting for transfers between devices, on_device(): lax.all_to_all(announcement(wave_pairs, lat_rows, devices), 'wave', 0, 0,...  2.98 us
  transfers between devices with their start and end apart: 2, of which 2 were waited for; matrix products, arithmetic and copies ran while one was open for 0% of the time, Pallas kernels for 13%

profile of v5, /device:TPU:6, one launch (start us, length us, event | category | flops | bytes accessed | tf_op | source)
XLA Modules:
  0.0 72.0 jit_solution(14074552024196245149)
XLA Ops:
  0.0 1.3 %shard_map.73 = f32[64,1,128]{2,1,0:T(1,128)} custom-call(s32[10]{0:T(128)} %waves.3, s32[4]{0:T(128)} %lat_rows.3), custom_call_target="tpu_custom_call" | custom-call | tf_op jit(solution)/shard_map/pallas_call | solution.py:96
  1.3 14.0 %all-to-all-start = ((f32[64,1,128]{2,1,0:T(1,128)}), f32[64,1,128]{2,1,0:T(1,128)S(1)}, u32[]{:S(2)}, u32[]{:S(2)}) async-start(f32[64,1,128]{2,1,0:T(1,128)} %shard_map.73), calls=%async_computation | async-start | bytes 65536 | tf_op jit(solution)/shard_map/all_to_all | solution.py:378
  15.3 0.0 copy-start.2
  15.4 0.0 copy-start.3
  15.4 4.5 %shard_map.74.sums_ref = f32[20,24,256]{2,1,0:T(8,128)S(1)} custom-call(s32[10]{0:T(128)} %waves.3, f32[10,10,2,1281]{3,2,1,0:T(2,128)} %bitcast.12, bf16[10,1281,128]{2,1,0:T(8,128)(2,1)} %leg_hbm.1), custom_call_target="tpu_custom_call" | custom-call | tf_op jit(solution)/shard_map/pallas_call | solution.py:71
  19.8 0.0 copy-start
  19.9 0.0 copy-start.1
  19.9 3.0 %all-to-all-done.index_ref = f32[64,1,128]{2,1,0:T(1,128)S(1)} async-done(((f32[64,1,128]{2,1,0:T(1,128)}), f32[64,1,128]{2,1,0:T(1,128)S(1)}, u32[]{:S(2)}, u32[]{:S(2)}) %all-to-all-start) | async-done | bytes 32800 | tf_op jit(solution)/shard_map/all_to_all | solution.py:378
  22.8 1.3 %shard_map.75 = bf16[64,16,128]{2,1,0:T(8,128)(2,1)} custom-call(f32[64,1,128]{2,1,0:T(1,128)S(1)} %all-to-all-done.index_ref, f32[20,24,256]{2,1,0:T(8,128)S(1)} %shard_map.74.sums_ref), custom_call_target="tpu_custom_call" | custom-call | tf_op jit(solution)/shard_map/pallas_call | solution.py:123
  24.1 7.4 %all-to-all-start.1 = ((bf16[64,16,128]{2,1,0:T(8,128)(2,1)}), bf16[64,16,128]{2,1,0:T(8,128)(2,1)S(1)}, u32[]{:S(2)}, u32[]{:S(2)}) async-start(bf16[64,16,128]{2,1,0:T(8,128)(2,1)} %shard_map.75), calls=%async_computation.1 | async-start | bytes 524288 | tf_op jit(solution)/shard_map/all_to_all | solution.py:381
  31.5 0.1 copy.10
  31.6 0.1 copy.11
  31.7 0.1 reshape.7.wave_ref
  31.8 0.0 copy-done.2
  31.8 0.0 copy-done.3
  31.8 4.9 %shard_map.76.table_ref = bf16[4,2560,128]{2,1,0:T(8,128)(2,1)S(1)} custom-call(s32[4]{0:T(128)S(1)} %copy-done.2, s32[256]{0:T(256)S(1)} %copy-done.3, f32[64,1,128]{2,1,0:T(1,128)S(1)} %all-to-all-done.index_ref), custom_call_target="tpu_custom_call" | custom-call | tf_op jit(solution)/shard_map/pallas_call | solution.py:185
  36.8 6.3 %all-to-all-done.1.got_ref = bf16[64,16,128]{2,1,0:T(8,128)(2,1)S(1)} async-done(((bf16[64,16,128]{2,1,0:T(8,128)(2,1)}), bf16[64,16,128]{2,1,0:T(8,128)(2,1)S(1)}, u32[]{:S(2)}, u32[]{:S(2)}) %all-to-all-start.1) | async-done | bytes 262176 | tf_op jit(solution)/shard_map/all_to_all | solution.py:381
  43.1 0.0 copy-done
  43.1 0.0 copy-done.1
  43.1 5.4 %shard_map.77 = bf16[8,208,128]{2,1,0:T(8,128)(2,1)S(1)} custom-call(s32[4]{0:T(128)S(1)} %copy-done.2, s32[256]{0:T(256)S(1)} %copy-done.3, bf16[64,16,128]{2,1,0:T(8,128)(2,1)S(1)} %all-to-all-done.1.got_ref, f32[1,1280]{1,0:T(1,128)S(1)} %reshape.7.wave_ref, bf16[240,128]{1,0:T(8,128)(2,1)S(1)} %copy-done, bf16[128,128]{1,0:T(8,128)(2,1)S(1)} %copy-done.1, ...), custom_call_target="tpu_custom_call" | custom-call | tf_op jit(solution)/shard_map/pallas_call | solution.py:323
  48.5 22.6 %all_to_all.15.in_ref = bf16[8,208,128]{2,1,0:T(8,128)(2,1)S(1)} all-to-all(bf16[8,208,128]{2,1,0:T(8,128)(2,1)S(1)} %shard_map.77), channel_id=1, replica_groups=mesh['wave'=64,'field'=8] {'field'}, dimensions={0} | all-to-all | bytes 851968 | tf_op jit(solution)/shard_map/all_to_all | solution.py:385
  71.1 1.0 %shard_map.78 = bf16[2,80,1289]{2,1,0:T(8,128)(2,1)} custom-call(bf16[8,208,128]{2,1,0:T(8,128)(2,1)S(1)} %all_to_all.15.in_ref), custom_call_target="tpu_custom_call" | custom-call | tf_op jit(solution)/shard_map/pallas_call | solution.py:355
  (4 shorter events, 0.0 us)
Async XLA Ops:
  1.3 21.5 %all-to-all-start = ((f32[64,1,128]{2,1,0:T(1,128)}), f32[64,1,128]{2,1,0:T(1,128)S(1)}, u32[]{:S(2)}, u32[]{:S(2)}) async-start(f32[64,1,128]{2,1,0:T(1,128)} %shard_map.73), calls=%async_computation | async-start | bytes 65536 | tf_op jit(solution)/shard_map/all_to_all | solution.py:378
  15.3 16.5 %copy-start.2 = (s32[4]{0:T(128)S(1)}, s32[4]{0:T(128)}, u32[]{:S(2)}) copy-start(s32[4]{0:T(128)} %lat_rows.3) | copy-start | bytes 52
  15.4 16.5 %copy-start.3 = (s32[256]{0:T(256)S(1)}, s32[256]{0:T(256)}, u32[]{:S(2)}) copy-start(s32[256]{0:T(256)} %npoints.3) | copy-start | bytes 3076
  19.8 23.2 %copy-start = (bf16[240,128]{1,0:T(8,128)(2,1)S(1)}, bf16[240,128]{1,0:T(8,128)(2,1)}, u32[]{:S(2)}) copy-start(bf16[240,128]{1,0:T(8,128)(2,1)} %constant.6.clone.select_ref) | copy-start | bytes 184324
  19.9 23.2 %copy-start.1 = (bf16[128,128]{1,0:T(8,128)(2,1)S(1)}, bf16[128,128]{1,0:T(8,128)(2,1)}, u32[]{:S(2)}) copy-start(bf16[128,128]{1,0:T(8,128)(2,1)} %constant.7.clone.reverse_ref) | copy-start | bytes 98308
  24.1 18.9 %all-to-all-start.1 = ((bf16[64,16,128]{2,1,0:T(8,128)(2,1)}), bf16[64,16,128]{2,1,0:T(8,128)(2,1)S(1)}, u32[]{:S(2)}, u32[]{:S(2)}) async-start(bf16[64,16,128]{2,1,0:T(8,128)(2,1)} %shard_map.75), calls=%async_computation.1 | async-start | bytes 524288 | tf_op jit(solution)/shard_map/all_to_all | solution.py:381

commit v6 on v5

--- a/solution.py
+++ b/solution.py
@@ -205,7 +205,7 @@
 
 
 def synthesis_kernel(
-    truncation, lat_rows, npoints, got_ref, wave_ref, select_ref, reverse_ref, table_ref, out_ref, got, parts, left, line, dense
+    truncation, lat_rows, npoints, got_ref, wave_ref, select_ref, reverse_ref, table_ref, out_ref, got, parts, left_0, left_1, line_0, line_1, dense
 ):
     devices = got_ref.shape[0]
     rows = TILES * devices
@@ -229,7 +229,9 @@
     place_in = lax.broadcasted_iota(i32, (BATCH, WIDTH), 0) * CHUNK + lax.broadcasted_iota(i32, (BATCH, WIDTH), 1)
     place_back = lax.broadcasted_iota(i32, (BATCH, WIDTH), 0) * CHUNK - lax.broadcasted_iota(i32, (BATCH, WIDTH), 1)
 
-    def batch(l, first, origin):
+    lefts, lines = (left_0, left_1), (line_0, line_1)
+
+    def rotate(left, l, first, origin):
         n = jnp.full((8, WIDTH), 2 * npoints[lat_rows[l]], i32).astype(f32)
         inverse = (1.0 / n)[0:1, 0:1]
         n = n[0:1, 0:1]
@@ -251,6 +253,8 @@
                 to = slice(f * BATCH, (f + 2) * BATCH)
                 left[to, at] = jnp.concatenate(turned_real, axis=0).astype(bf16)
                 left[to, at_imag] = jnp.concatenate(turned_imag, axis=0).astype(bf16)
+
+    def multiply(left, line, l, first, origin):
         even = jnp.dot(left[:, 0:depth], table_ref[l, 0:depth], preferred_element_type=f32)
         odd = jnp.dot(left[:, depth : 2 * depth], table_ref[l, depth : 2 * depth], preferred_element_type=f32)
         before, after = even + odd, even - odd
@@ -264,24 +268,29 @@
             to = pl.ds(pl.multiple_of((COLUMNS + f) * chunks + first, 8), BATCH)
             line[to] = jnp.where(keep_in, after[at], line[to])
 
+    def body(step, carry):
+        at = []
+        for pair in range(2):
+            n_a = npoints[lat_rows[2 * pair]]
+            batches_a = lax.shift_right_arithmetic(n_a - 1, 11) + 1
+            start_b = lax.shift_right_arithmetic(n_a, 11)
+            second = step >= batches_a
+            index = jnp.where(second, jnp.minimum(step - batches_a + start_b, BATCHES - 1), step)
+            at.append((2 * pair + jnp.where(second, 1, 0), BATCH * index, jnp.where(second, n_a, 0)))
+        for pair in range(2):
+            rotate(lefts[pair], *at[pair])
+        for pair in range(2):
+            multiply(lefts[pair], lines[pair], *at[pair])
+        return carry
+
+    lax.fori_loop(0, BATCHES + 1, body, 0, unroll=True)
     lane = lax.broadcasted_iota(i32, (COLUMNS, WIDTH), 1)
     for pair in range(2):
-        n_a = npoints[lat_rows[2 * pair]]
-        batches_a = lax.shift_right_arithmetic(n_a - 1, 11) + 1
-        start_b = lax.shift_right_arithmetic(n_a, 11)
-
-        def body(step, carry):
-            second = step >= batches_a
-            l = 2 * pair + jnp.where(second, 1, 0)
-            first = BATCH * jnp.where(second, step - batches_a + start_b, step)
-            batch(l, first, jnp.where(second, n_a, 0))
-            return carry
-
-        lax.fori_loop(0, batches_a + BATCHES - start_b, body, 0)
+        line = lines[pair]
         back = slice(0, COLUMNS * chunks)
         line[back] = jnp.dot(line[back].astype(bf16), reverse_ref[...], preferred_element_type=f32)
 
-        def tile_of(tile):
+        def tile_of(tile, line=line):
             return line[pl.ds((tile % 2) * COLUMNS * chunks + tile // 2, COLUMNS, chunks), :]
 
         for q in range(4):
@@ -329,6 +338,8 @@
             pltpu.VMEM((devices * 4 * TILES, WIDTH), f32),
             pltpu.VMEM((4, 2, ROWS, depth), f32),
             pltpu.VMEM((BATCH * COLUMNS, 2 * depth), bf16),
+            pltpu.VMEM((BATCH * COLUMNS, 2 * depth), bf16),
+            pltpu.VMEM((2 * COLUMNS * BATCH * BATCHES, WIDTH), f32),
             pltpu.VMEM((2 * COLUMNS * BATCH * BATCHES, WIDTH), f32),
             pltpu.VMEM((4, DENSE, WIDTH), f32),
         ],

time: 72.3 us -> 71.2 us (0.985)
  Pallas kernels: 18.4 us -> 17.3 us
    pallas_call x1, Pallas kernels: 5.42 us -> 4.32 us  [synthesis(): pl.pallas_call(functools.partial(synthesis_kernel, float(truncation)), ou...]
where the time goes in v6:
time: 71.2 us; the launch traced here: 70.9 us
  blocking collectives  22.6 us (32%)
  starting transfers between devices  21.4 us (30%)
  Pallas kernels  17.3 us (24%)
  waiting for transfers between devices  9.29 us (13%)
    all_to_all x1, blocking collectives, on_device(): return place(lax.all_to_all(blocks, 'field', 0, 0, tiled=True))  22.6 us
    all_to_all x1, starting transfers between devices, on_device(): lax.all_to_all(announcement(wave_pairs, lat_rows, devices), 'wave', 0, 0,...  14 us
    all_to_all x1, starting transfers between devices, on_device(): received = lax.all_to_all(ordered, 'wave', 0, 0, tiled=True)  7.35 us
    all_to_all x1, waiting for transfers between devices, on_device(): received = lax.all_to_all(ordered, 'wave', 0, 0, tiled=True)  6.31 us
    pallas_call x1, Pallas kernels, fourier_tables(): pl.pallas_call(functools.partial(table_kernel, float(truncation)), out_sh...  4.93 us
    pallas_call x1, Pallas kernels, legendre_sums(): pl.pallas_call(functools.partial(legendre_kernel, rows - 2), out_shape=pl...  4.46 us
    pallas_call x1, Pallas kernels, synthesis(): pl.pallas_call(functools.partial(synthesis_kernel, float(truncation)), ou...  4.32 us
    all_to_all x1, waiting for transfers between devices, on_device(): lax.all_to_all(announcement(wave_pairs, lat_rows, devices), 'wave', 0, 0,...  2.98 us
  transfers between devices with their start and end apart: 2, of which 2 were waited for; matrix products, arithmetic and copies ran while one was open for 0% of the time, Pallas kernels for 13%

profile of v6, /device:TPU:6, one launch (start us, length us, event | category | flops | bytes accessed | tf_op | source)
XLA Modules:
  0.0 70.9 jit_solution(14457036392338248476)
XLA Ops:
  0.0 1.3 %shard_map.73 = f32[64,1,128]{2,1,0:T(1,128)} custom-call(s32[10]{0:T(128)} %waves.3, s32[4]{0:T(128)} %lat_rows.3), custom_call_target="tpu_custom_call" | custom-call | tf_op jit(solution)/shard_map/pallas_call | solution.py:96
  1.3 14.0 %all-to-all-start = ((f32[64,1,128]{2,1,0:T(1,128)}), f32[64,1,128]{2,1,0:T(1,128)S(1)}, u32[]{:S(2)}, u32[]{:S(2)}) async-start(f32[64,1,128]{2,1,0:T(1,128)} %shard_map.73), calls=%async_computation | async-start | bytes 65536 | tf_op jit(solution)/shard_map/all_to_all | solution.py:389
  15.3 0.0 copy-start.2
  15.4 0.0 copy-start.3
  15.4 4.5 %shard_map.74.sums_ref = f32[20,24,256]{2,1,0:T(8,128)S(1)} custom-call(s32[10]{0:T(128)} %waves.3, f32[10,10,2,1281]{3,2,1,0:T(2,128)} %bitcast.12, bf16[10,1281,128]{2,1,0:T(8,128)(2,1)} %leg_hbm.1), custom_call_target="tpu_custom_call" | custom-call | tf_op jit(solution)/shard_map/pallas_call | solution.py:71
  19.8 0.0 copy-start
  19.9 0.0 copy-start.1
  19.9 3.0 %all-to-all-done.index_ref = f32[64,1,128]{2,1,0:T(1,128)S(1)} async-done(((f32[64,1,128]{2,1,0:T(1,128)}), f32[64,1,128]{2,1,0:T(1,128)S(1)}, u32[]{:S(2)}, u32[]{:S(2)}) %all-to-all-start) | async-done | bytes 32800 | tf_op jit(solution)/shard_map/all_to_all | solution.py:389
  22.8 1.3 %shard_map.75 = bf16[64,16,128]{2,1,0:T(8,128)(2,1)} custom-call(f32[64,1,128]{2,1,0:T(1,128)S(1)} %all-to-all-done.index_ref, f32[20,24,256]{2,1,0:T(8,128)S(1)} %shard_map.74.sums_ref), custom_call_target="tpu_custom_call" | custom-call | tf_op jit(solution)/shard_map/pallas_call | solution.py:123
  24.1 7.4 %all-to-all-start.1 = ((bf16[64,16,128]{2,1,0:T(8,128)(2,1)}), bf16[64,16,128]{2,1,0:T(8,128)(2,1)S(1)}, u32[]{:S(2)}, u32[]{:S(2)}) async-start(bf16[64,16,128]{2,1,0:T(8,128)(2,1)} %shard_map.75), calls=%async_computation.1 | async-start | bytes 524288 | tf_op jit(solution)/shard_map/all_to_all | solution.py:392
  31.5 0.1 copy.10
  31.6 0.1 copy.11
  31.7 0.1 reshape.7.wave_ref
  31.8 0.0 copy-done.2
  31.8 0.0 copy-done.3
  31.8 4.9 %shard_map.76.table_ref = bf16[4,2560,128]{2,1,0:T(8,128)(2,1)S(1)} custom-call(s32[4]{0:T(128)S(1)} %copy-done.2, s32[256]{0:T(256)S(1)} %copy-done.3, f32[64,1,128]{2,1,0:T(1,128)S(1)} %all-to-all-done.index_ref), custom_call_target="tpu_custom_call" | custom-call | tf_op jit(solution)/shard_map/pallas_call | solution.py:185
  36.8 6.3 %all-to-all-done.1.got_ref = bf16[64,16,128]{2,1,0:T(8,128)(2,1)S(1)} async-done(((bf16[64,16,128]{2,1,0:T(8,128)(2,1)}), bf16[64,16,128]{2,1,0:T(8,128)(2,1)S(1)}, u32[]{:S(2)}, u32[]{:S(2)}) %all-to-all-start.1) | async-done | bytes 262176 | tf_op jit(solution)/shard_map/all_to_all | solution.py:392
  43.1 0.0 copy-done
  43.1 0.0 copy-done.1
  43.1 4.3 %shard_map.77 = bf16[8,208,128]{2,1,0:T(8,128)(2,1)S(1)} custom-call(s32[4]{0:T(128)S(1)} %copy-done.2, s32[256]{0:T(256)S(1)} %copy-done.3, bf16[64,16,128]{2,1,0:T(8,128)(2,1)S(1)} %all-to-all-done.1.got_ref, f32[1,1280]{1,0:T(1,128)S(1)} %reshape.7.wave_ref, bf16[240,128]{1,0:T(8,128)(2,1)S(1)} %copy-done, bf16[128,128]{1,0:T(8,128)(2,1)S(1)} %copy-done.1, ...), custom_call_target="tpu_custom_call" | custom-call | tf_op jit(solution)/shard_map/pallas_call | solution.py:332
  47.4 22.6 %all_to_all.15.in_ref = bf16[8,208,128]{2,1,0:T(8,128)(2,1)S(1)} all-to-all(bf16[8,208,128]{2,1,0:T(8,128)(2,1)S(1)} %shard_map.77), channel_id=1, replica_groups=mesh['wave'=64,'field'=8] {'field'}, dimensions={0} | all-to-all | bytes 851968 | tf_op jit(solution)/shard_map/all_to_all | solution.py:396
  70.0 1.0 %shard_map.78 = bf16[2,80,1289]{2,1,0:T(8,128)(2,1)} custom-call(bf16[8,208,128]{2,1,0:T(8,128)(2,1)S(1)} %all_to_all.15.in_ref), custom_call_target="tpu_custom_call" | custom-call | tf_op jit(solution)/shard_map/pallas_call | solution.py:366
  (4 shorter events, 0.0 us)
Async XLA Ops:
  1.3 21.5 %all-to-all-start = ((f32[64,1,128]{2,1,0:T(1,128)}), f32[64,1,128]{2,1,0:T(1,128)S(1)}, u32[]{:S(2)}, u32[]{:S(2)}) async-start(f32[64,1,128]{2,1,0:T(1,128)} %shard_map.73), calls=%async_computation | async-start | bytes 65536 | tf_op jit(solution)/shard_map/all_to_all | solution.py:389
  15.3 16.5 %copy-start.2 = (s32[4]{0:T(128)S(1)}, s32[4]{0:T(128)}, u32[]{:S(2)}) copy-start(s32[4]{0:T(128)} %lat_rows.3) | copy-start | bytes 52
  15.4 16.5 %copy-start.3 = (s32[256]{0:T(256)S(1)}, s32[256]{0:T(256)}, u32[]{:S(2)}) copy-start(s32[256]{0:T(256)} %npoints.3) | copy-start | bytes 3076
  19.8 23.2 %copy-start = (bf16[240,128]{1,0:T(8,128)(2,1)S(1)}, bf16[240,128]{1,0:T(8,128)(2,1)}, u32[]{:S(2)}) copy-start(bf16[240,128]{1,0:T(8,128)(2,1)} %constant.6.clone.select_ref) | copy-start | bytes 184324
  19.9 23.2 %copy-start.1 = (bf16[128,128]{1,0:T(8,128)(2,1)S(1)}, bf16[128,128]{1,0:T(8,128)(2,1)}, u32[]{:S(2)}) copy-start(bf16[128,128]{1,0:T(8,128)(2,1)} %constant.7.clone.reverse_ref) | copy-start | bytes 98308
  24.1 18.9 %all-to-all-start.1 = ((bf16[64,16,128]{2,1,0:T(8,128)(2,1)}), bf16[64,16,128]{2,1,0:T(8,128)(2,1)S(1)}, u32[]{:S(2)}, u32[]{:S(2)}) async-start(bf16[64,16,128]{2,1,0:T(8,128)(2,1)} %shard_map.75), calls=%async_computation.1 | async-start | bytes 524288 | tf_op jit(solution)/shard_map/all_to_all | solution.py:392

commit v7 on v6

--- a/solution.py
+++ b/solution.py
@@ -147,7 +147,7 @@
 BLOCK = 128
 
 
-def table_kernel(truncation, lat_rows, npoints, index_ref, out_ref, waves):
+def table_kernel(truncation, lat_rows, npoints, index_ref, out_ref, points_ref, waves):
     l = pl.program_id(0)
     devices = index_ref.shape[0]
     depth = GROUPS * TILES * devices
@@ -164,6 +164,7 @@
                 at = devices * (TILES * g + t)
                 waves[at : at + devices, :] = jnp.broadcast_to(column, (devices, 128))
 
+    points_ref[l] = npoints[lat_rows[l]]
     odd = (2 * lax.broadcasted_iota(i32, (BLOCK, 128), 1) + 1).astype(f32)
     n = jnp.full((8, 128), 2 * npoints[lat_rows[l]], i32).astype(f32)
     inverse = (1.0 / n)[0:1]
@@ -184,12 +185,15 @@
     depth = GROUPS * TILES * devices
     return pl.pallas_call(
         functools.partial(table_kernel, float(truncation)),
-        out_shape=pltpu.VMEM((4, 2 * depth, CHUNK // 2), bf16),
+        out_shape=(pltpu.VMEM((4, 2 * depth, CHUNK // 2), bf16), jax.ShapeDtypeStruct((4,), i32)),
         grid_spec=pltpu.PrefetchScalarGridSpec(
             num_scalar_prefetch=2,
             grid=(4,),
             in_specs=[VMEM_SPEC],
-            out_specs=pl.BlockSpec((1, 2 * depth, CHUNK // 2), lambda l, a, b: (l, 0, 0)),
+            out_specs=(
+                pl.BlockSpec((1, 2 * depth, CHUNK // 2), lambda l, a, b: (l, 0, 0)),
+                pl.BlockSpec(memory_space=pltpu.SMEM),
+            ),
             scratch_shapes=[pltpu.VMEM((depth, 128), f32)],
         ),
         compiler_params=pltpu.CompilerParams(vmem_limit_bytes=8 << 20),
@@ -205,7 +209,7 @@
 
 
 def synthesis_kernel(
-    truncation, lat_rows, npoints, got_ref, wave_ref, select_ref, reverse_ref, table_ref, out_ref, got, parts, left_0, left_1, line_0, line_1, dense
+    truncation, points, got_ref, wave_ref, select_ref, reverse_ref, table_ref, out_ref, got, parts, left_0, left_1, line_0, line_1, dense
 ):
     devices = got_ref.shape[0]
     rows = TILES * devices
@@ -232,7 +236,7 @@
     lefts, lines = (left_0, left_1), (line_0, line_1)
 
     def rotate(left, l, first, origin):
-        n = jnp.full((8, WIDTH), 2 * npoints[lat_rows[l]], i32).astype(f32)
+        n = jnp.full((8, WIDTH), 2 * points[l], i32).astype(f32)
         inverse = (1.0 / n)[0:1, 0:1]
         n = n[0:1, 0:1]
         center = (2 * CHUNK * (first + chunk) - 2 * origin + CHUNK - 1).astype(f32)
@@ -271,7 +275,7 @@
     def body(step, carry):
         at = []
         for pair in range(2):
-            n_a = npoints[lat_rows[2 * pair]]
+            n_a = points[2 * pair]
             batches_a = lax.shift_right_arithmetic(n_a - 1, 11) + 1
             start_b = lax.shift_right_arithmetic(n_a, 11)
             second = step >= batches_a
@@ -295,15 +299,17 @@
 
         for q in range(4):
             shift = (QUARTER * q) % WIDTH
+            first = QUARTER * q // WIDTH
+            ahead = tile_of(first)
+            if shift:
+                ahead = pltpu.roll(ahead, WIDTH - shift, 1)
             for i in range(QUARTER // WIDTH + 1):
-                tile = QUARTER * q // WIDTH + i
-                v = tile_of(tile)
+                v = ahead
+                if shift or i < QUARTER // WIDTH:
+                    ahead = tile_of(first + i + 1)
                 if shift:
-                    v = jnp.where(
-                        lane < WIDTH - shift,
-                        pltpu.roll(v, WIDTH - shift, 1),
-                        pltpu.roll(tile_of(tile + 1), WIDTH - shift, 1),
-                    )
+                    ahead = pltpu.roll(ahead, WIDTH - shift, 1)
+                    v = jnp.where(lane < WIDTH - shift, v, ahead)
                 if i < 10:
                     dense[q, COLUMNS * i : COLUMNS * i + COLUMNS] = v
                 else:
@@ -325,14 +331,14 @@
     return table.reshape(GROUPS * 2 * ROWS, 128).astype(jnp.bfloat16)
 
 
-def synthesis(lat_rows, npoints, received, wave_line, tables, truncation):
+def synthesis(points, received, wave_line, tables, truncation):
     devices = received.shape[0]
     depth = GROUPS * TILES * devices
     reverse = np.eye(WIDTH)[::-1].astype(jnp.bfloat16)
     return pl.pallas_call(
         functools.partial(synthesis_kernel, float(truncation)),
         out_shape=jax.ShapeDtypeStruct((8, DENSE, WIDTH), bf16),
-        in_specs=[pl.BlockSpec(memory_space=pltpu.SMEM)] * 2 + [VMEM_SPEC] * 5,
+        in_specs=[pl.BlockSpec(memory_space=pltpu.SMEM)] + [VMEM_SPEC] * 5,
         out_specs=VMEM_SPEC,
         scratch_shapes=[
             pltpu.VMEM((devices * 4 * TILES, WIDTH), f32),
@@ -344,7 +350,7 @@
             pltpu.VMEM((4, DENSE, WIDTH), f32),
         ],
         compiler_params=pltpu.CompilerParams(vmem_limit_bytes=16 << 20),
-    )(lat_rows, npoints, received, wave_line, select_rows(), reverse, tables)
+    )(points, received, wave_line, select_rows(), reverse, tables)
 
 
 def place_kernel(in_ref, out_ref, dense, placed):
@@ -390,9 +396,9 @@
     sums = legendre_sums(wave_pairs, spectral, legendre)
     ordered = order_latitudes(index, sums)
     received = lax.all_to_all(ordered, "wave", 0, 0, tiled=True)
-    tables = fourier_tables(lat_rows, npoints, index, truncation)
+    tables, points = fourier_tables(lat_rows, npoints, index, truncation)
     wave_line = wave_line_of(index, float(truncation))
-    blocks = synthesis(lat_rows, npoints, received, wave_line, tables, truncation)
+    blocks = synthesis(points, received, wave_line, tables, truncation)
     return place(lax.all_to_all(blocks, "field", 0, 0, tiled=True))
 
 

time: 71.2 us -> 71.1 us (level)
  transfers between devices with their start and end apart: 2 -> 2, of which waited for: 2 -> 2; matrix products, arithmetic and copies ran while one was open for 0% -> 0% of each run, Pallas kernels for 13% -> 14%
where the time goes in v7:
time: 71.1 us; the launch traced here: 70.8 us
  blocking collectives  22.6 us (32%)
  starting transfers between devices  21.4 us (30%)
  Pallas kernels  17.8 us (25%)
  waiting for transfers between devices  8.65 us (12%)
    all_to_all x1, blocking collectives, on_device(): return place(lax.all_to_all(blocks, 'field', 0, 0, tiled=True))  22.6 us
    all_to_all x1, starting transfers between devices, on_device(): lax.all_to_all(announcement(wave_pairs, lat_rows, devices), 'wave', 0, 0,...  14 us
    all_to_all x1, starting transfers between devices, on_device(): received = lax.all_to_all(ordered, 'wave', 0, 0, tiled=True)  7.35 us
    all_to_all x1, waiting for transfers between devices, on_device(): received = lax.all_to_all(ordered, 'wave', 0, 0, tiled=True)  5.67 us
    pallas_call x1, Pallas kernels, fourier_tables(): pl.pallas_call(functools.partial(table_kernel, float(truncation)), out_sh...  5.57 us
    pallas_call x1, Pallas kernels, legendre_sums(): pl.pallas_call(functools.partial(legendre_kernel, rows - 2), out_shape=pl...  4.46 us
    pallas_call x1, Pallas kernels, synthesis(): pl.pallas_call(functools.partial(synthesis_kernel, float(truncation)), ou...  4.23 us
    all_to_all x1, waiting for transfers between devices, on_device(): lax.all_to_all(announcement(wave_pairs, lat_rows, devices), 'wave', 0, 0,...  2.98 us
  transfers between devices with their start and end apart: 2, of which 2 were waited for; matrix products, arithmetic and copies ran while one was open for 0% of the time, Pallas kernels for 14%

profile of v7, /device:TPU:6, one launch (start us, length us, event | category | flops | bytes accessed | tf_op | source)
XLA Modules:
  0.0 70.8 jit_solution(8434330860205505762)
XLA Ops:
  0.0 1.3 %shard_map.73 = f32[64,1,128]{2,1,0:T(1,128)} custom-call(s32[10]{0:T(128)} %waves.3, s32[4]{0:T(128)} %lat_rows.1), custom_call_target="tpu_custom_call" | custom-call | tf_op jit(solution)/shard_map/pallas_call | solution.py:96
  1.3 14.0 %all-to-all-start = ((f32[64,1,128]{2,1,0:T(1,128)}), f32[64,1,128]{2,1,0:T(1,128)S(1)}, u32[]{:S(2)}, u32[]{:S(2)}) async-start(f32[64,1,128]{2,1,0:T(1,128)} %shard_map.73), calls=%async_computation | async-start | bytes 65536 | tf_op jit(solution)/shard_map/all_to_all | solution.py:395
  15.3 0.0 copy-start.2
  15.4 0.0 copy-start.3
  15.4 0.0 copy-start
  15.4 0.0 copy-start.1
  15.4 4.5 %shard_map.75.sums_ref = f32[20,24,256]{2,1,0:T(8,128)S(1)} custom-call(s32[10]{0:T(128)} %waves.3, f32[10,10,2,1281]{3,2,1,0:T(2,128)} %bitcast.12, bf16[10,1281,128]{2,1,0:T(8,128)(2,1)} %leg_hbm.1), custom_call_target="tpu_custom_call" | custom-call | tf_op jit(solution)/shard_map/pallas_call | solution.py:71
  19.9 3.0 %all-to-all-done.index_ref = f32[64,1,128]{2,1,0:T(1,128)S(1)} async-done(((f32[64,1,128]{2,1,0:T(1,128)}), f32[64,1,128]{2,1,0:T(1,128)S(1)}, u32[]{:S(2)}, u32[]{:S(2)}) %all-to-all-start) | async-done | bytes 32800 | tf_op jit(solution)/shard_map/all_to_all | solution.py:395
  22.8 1.3 %shard_map.76 = bf16[64,16,128]{2,1,0:T(8,128)(2,1)} custom-call(f32[64,1,128]{2,1,0:T(1,128)S(1)} %all-to-all-done.index_ref, f32[20,24,256]{2,1,0:T(8,128)S(1)} %shard_map.75.sums_ref), custom_call_target="tpu_custom_call" | custom-call | tf_op jit(solution)/shard_map/pallas_call | solution.py:123
  24.1 7.4 %all-to-all-start.1 = ((bf16[64,16,128]{2,1,0:T(8,128)(2,1)}), bf16[64,16,128]{2,1,0:T(8,128)(2,1)S(1)}, u32[]{:S(2)}, u32[]{:S(2)}) async-start(bf16[64,16,128]{2,1,0:T(8,128)(2,1)} %shard_map.76), calls=%async_computation.1 | async-start | bytes 524288 | tf_op jit(solution)/shard_map/all_to_all | solution.py:398
  31.5 0.1 copy.10
  31.6 0.1 copy.11
  31.7 0.1 reshape.7.wave_ref
  31.8 0.0 copy-done.2
  31.8 0.0 copy-done.3
  31.8 5.6 %shard_map.74 = (bf16[4,2560,128]{2,1,0:T(8,128)(2,1)S(1)}, s32[4]{0:T(128)S(1)}) custom-call(s32[4]{0:T(128)S(1)} %copy-done.2, s32[256]{0:T(256)S(1)} %copy-done.3, f32[64,1,128]{2,1,0:T(1,128)S(1)} %all-to-all-done.index_ref), custom_call_target="tpu_custom_call" | custom-call | tf_op jit(solution)/shard_map/pallas_call | solution.py:186
  37.4 5.7 %all-to-all-done.1.got_ref = bf16[64,16,128]{2,1,0:T(8,128)(2,1)S(1)} async-done(((bf16[64,16,128]{2,1,0:T(8,128)(2,1)}), bf16[64,16,128]{2,1,0:T(8,128)(2,1)S(1)}, u32[]{:S(2)}, u32[]{:S(2)}) %all-to-all-start.1) | async-done | bytes 262176 | tf_op jit(solution)/shard_map/all_to_all | solution.py:398
  43.1 0.0 copy-done
  43.1 0.0 copy-done.1
  43.1 4.2 %shard_map.77 = bf16[8,208,128]{2,1,0:T(8,128)(2,1)S(1)} custom-call(s32[4]{0:T(128)S(1)} %get-tuple-element.7.points, bf16[64,16,128]{2,1,0:T(8,128)(2,1)S(1)} %all-to-all-done.1.got_ref, f32[1,1280]{1,0:T(1,128)S(1)} %reshape.7.wave_ref, bf16[240,128]{1,0:T(8,128)(2,1)S(1)} %copy-done, bf16[128,128]{1,0:T(8,128)(2,1)S(1)} %copy-done.1, ...), custom_call_target="tpu_custom_call" | custom-call | tf_op jit(solution)/shard_map/pallas_call | solution.py:338
  47.3 22.6 %all_to_all.15.in_ref = bf16[8,208,128]{2,1,0:T(8,128)(2,1)S(1)} all-to-all(bf16[8,208,128]{2,1,0:T(8,128)(2,1)S(1)} %shard_map.77), channel_id=1, replica_groups=mesh['wave'=64,'field'=8] {'field'}, dimensions={0} | all-to-all | bytes 851968 | tf_op jit(solution)/shard_map/all_to_all | solution.py:402
  69.9 1.0 %shard_map.78 = bf16[2,80,1289]{2,1,0:T(8,128)(2,1)} custom-call(bf16[8,208,128]{2,1,0:T(8,128)(2,1)S(1)} %all_to_all.15.in_ref), custom_call_target="tpu_custom_call" | custom-call | tf_op jit(solution)/shard_map/pallas_call | solution.py:372
  (4 shorter events, 0.0 us)
Async XLA Ops:
  1.3 21.5 %all-to-all-start = ((f32[64,1,128]{2,1,0:T(1,128)}), f32[64,1,128]{2,1,0:T(1,128)S(1)}, u32[]{:S(2)}, u32[]{:S(2)}) async-start(f32[64,1,128]{2,1,0:T(1,128)} %shard_map.73), calls=%async_computation | async-start | bytes 65536 | tf_op jit(solution)/shard_map/all_to_all | solution.py:395
  15.3 16.5 %copy-start.2 = (s32[4]{0:T(128)S(1)}, s32[4]{0:T(128)}, u32[]{:S(2)}) copy-start(s32[4]{0:T(128)} %lat_rows.1) | copy-start | bytes 52
  15.4 16.5 %copy-start.3 = (s32[256]{0:T(256)S(1)}, s32[256]{0:T(256)}, u32[]{:S(2)}) copy-start(s32[256]{0:T(256)} %npoints.1) | copy-start | bytes 3076
  15.4 27.7 %copy-start = (bf16[240,128]{1,0:T(8,128)(2,1)S(1)}, bf16[240,128]{1,0:T(8,128)(2,1)}, u32[]{:S(2)}) copy-start(bf16[240,128]{1,0:T(8,128)(2,1)} %constant.6.clone.select_ref) | copy-start | bytes 184324
  15.4 27.7 %copy-start.1 = (bf16[128,128]{1,0:T(8,128)(2,1)S(1)}, bf16[128,128]{1,0:T(8,128)(2,1)}, u32[]{:S(2)}) copy-start(bf16[128,128]{1,0:T(8,128)(2,1)} %constant.7.clone.reverse_ref) | copy-start | bytes 98308
  24.1 18.9 %all-to-all-start.1 = ((bf16[64,16,128]{2,1,0:T(8,128)(2,1)}), bf16[64,16,128]{2,1,0:T(8,128)(2,1)S(1)}, u32[]{:S(2)}, u32[]{:S(2)}) async-start(bf16[64,16,128]{2,1,0:T(8,128)(2,1)} %shard_map.76), calls=%async_computation.1 | async-start | bytes 524288 | tf_op jit(solution)/shard_map/all_to_all | solution.py:398

commit v8 on v7

--- a/solution.py
+++ b/solution.py
@@ -20,7 +20,7 @@
 VMEM_SPEC = pl.BlockSpec(memory_space=pltpu.VMEM)
 
 
-def legendre_kernel(truncation, waves, spec_hbm, leg_hbm, out_ref, spec_ref, leg_ref, coeffs, spec_sems, leg_sems):
+def legendre_kernel(truncation, waves, spec_hbm, leg_hbm, out_ref, spec_ref, leg_ref, coeffs, found, spec_sems, leg_sems):
     rows = truncation + 2
     slots, fields = spec_ref.shape[0], spec_ref.shape[1]
     main = rows - 1
@@ -57,10 +57,15 @@
         for half in range(2):
             for side in range(2):
                 at = (2 * half + side) * ROWS
-                out_ref[2 * slot + half, :, 128 * side : 128 * side + 128] = sums[at : at + ROWS, :]
+                found[2 * slot + half, :, 128 * side : 128 * side + 128] = sums[at : at + ROWS, :]
         return carry
 
     lax.fori_loop(0, slots, body, 0)
+    lats = found.shape[2]
+    for t in range(TILES):
+        part = found[GROUPS * t : GROUPS * (t + 1)].reshape(GROUPS * ROWS, lats)
+        part = jnp.concatenate([part, jnp.zeros((128 - GROUPS * ROWS, lats), f32)], axis=0)
+        out_ref[:, 128 * t : 128 * t + 128] = jnp.transpose(part).astype(bf16)
 
 
 def legendre_sums(wave_pairs, spectral, legendre):
@@ -70,13 +75,14 @@
     legendre = pltpu.with_memory_space_constraint(legendre, pltpu.HBM)
     return pl.pallas_call(
         functools.partial(legendre_kernel, rows - 2),
-        out_shape=pltpu.VMEM((2 * slots, ROWS, 2 * northern), f32),
+        out_shape=pltpu.VMEM((2 * northern, 128 * TILES), bf16),
         in_specs=[pl.BlockSpec(memory_space=pltpu.SMEM)] + [pl.BlockSpec(memory_space=pltpu.HBM)] * 2,
         out_specs=VMEM_SPEC,
         scratch_shapes=[
             pltpu.VMEM((slots, fields, 2, rows), f32),
             pltpu.VMEM((slots, rows, northern), bf16),
             pltpu.VMEM((ROWS, 1408), f32),
+            pltpu.VMEM((2 * slots, ROWS, 2 * northern), f32),
             pltpu.SemaphoreType.DMA((slots,)),
             pltpu.SemaphoreType.DMA((slots,)),
         ],
@@ -103,16 +109,14 @@
 
 
 def order_kernel(index_ref, sums_ref, out_ref, scratch):
-    devices, lats = index_ref.shape[0], sums_ref.shape[2]
+    devices, lats = index_ref.shape[0], sums_ref.shape[0]
     index = index_ref[:, 0, :]
     lane = lax.broadcasted_iota(i32, (devices, lats), 1).astype(f32)
     onehot = jnp.concatenate(
         [jnp.where(index[:, 10 + j : 11 + j] == lane, 1.0, 0.0) for j in range(4)], axis=0
     ).astype(bf16)
     for t in range(TILES):
-        part = sums_ref[GROUPS * t : GROUPS * (t + 1)].reshape(GROUPS * ROWS, lats)
-        part = jnp.concatenate([part, jnp.zeros((128 - GROUPS * ROWS, lats), f32)], axis=0).astype(bf16)
-        picked = lax.dot_general(onehot, part, (((1,), (1,)), ((), ())), preferred_element_type=f32)
+        picked = jnp.dot(onehot, sums_ref[:, 128 * t : 128 * t + 128], preferred_element_type=f32)
         for j in range(4):
             scratch[pl.ds(j * TILES + t, devices, 4 * TILES), :] = picked[devices * j : devices * (j + 1), :]
     out_ref[...] = scratch[...].reshape(out_ref.shape).astype(bf16)

time: 71.1 us -> 71.3 us (level)
  no operation moved by 1% of the time
where the time goes in v8:
time: 71.3 us; the launch traced here: 71 us
  blocking collectives  22.6 us (32%)
  starting transfers between devices  21.5 us (30%)
  Pallas kernels  18 us (25%)
  waiting for transfers between devices  8.51 us (12%)
    all_to_all x1, blocking collectives, on_device(): return place(lax.all_to_all(blocks, 'field', 0, 0, tiled=True))  22.6 us
    all_to_all x1, starting transfers between devices, on_device(): lax.all_to_all(announcement(wave_pairs, lat_rows, devices), 'wave', 0, 0,...  14 us
    all_to_all x1, starting transfers between devices, on_device(): received = lax.all_to_all(ordered, 'wave', 0, 0, tiled=True)  7.49 us
    all_to_all x1, waiting for transfers between devices, on_device(): received = lax.all_to_all(ordered, 'wave', 0, 0, tiled=True)  5.67 us
    pallas_call x1, Pallas kernels, fourier_tables(): pl.pallas_call(functools.partial(table_kernel, float(truncation)), out_sh...  5.57 us
    pallas_call x1, Pallas kernels, legendre_sums(): pl.pallas_call(functools.partial(legendre_kernel, rows - 2), out_shape=pl...  4.6 us
    pallas_call x1, Pallas kernels, synthesis(): pl.pallas_call(functools.partial(synthesis_kernel, float(truncation)), ou...  4.23 us
    all_to_all x1, waiting for transfers between devices, on_device(): lax.all_to_all(announcement(wave_pairs, lat_rows, devices), 'wave', 0, 0,...  2.84 us
  transfers between devices with their start and end apart: 2, of which 2 were waited for; matrix products, arithmetic and copies ran while one was open for 0% of the time, Pallas kernels for 14%

profile of v8, /device:TPU:6, one launch (start us, length us, event | category | flops | bytes accessed | tf_op | source)
XLA Modules:
  0.0 71.0 jit_solution(18008239946394470868)
XLA Ops:
  0.0 1.3 %shard_map.73 = f32[64,1,128]{2,1,0:T(1,128)} custom-call(s32[10]{0:T(128)} %waves.3, s32[4]{0:T(128)} %lat_rows.1), custom_call_target="tpu_custom_call" | custom-call | tf_op jit(solution)/shard_map/pallas_call | solution.py:102
  1.3 14.0 %all-to-all-start = ((f32[64,1,128]{2,1,0:T(1,128)}), f32[64,1,128]{2,1,0:T(1,128)S(1)}, u32[]{:S(2)}, u32[]{:S(2)}) async-start(f32[64,1,128]{2,1,0:T(1,128)} %shard_map.73), calls=%async_computation | async-start | bytes 65536 | tf_op jit(solution)/shard_map/all_to_all | solution.py:399
  15.3 0.0 copy-start.2
  15.4 0.0 copy-start.3
  15.4 0.0 copy-start
  15.4 0.0 copy-start.1
  15.4 4.6 %shard_map.75.sums_ref = bf16[256,512]{1,0:T(8,128)(2,1)S(1)} custom-call(s32[10]{0:T(128)} %waves.3, f32[10,10,2,1281]{3,2,1,0:T(2,128)} %bitcast.12, bf16[10,1281,128]{2,1,0:T(8,128)(2,1)} %leg_hbm.1), custom_call_target="tpu_custom_call" | custom-call | tf_op jit(solution)/shard_map/pallas_call | solution.py:76
  20.0 2.8 %all-to-all-done.index_ref = f32[64,1,128]{2,1,0:T(1,128)S(1)} async-done(((f32[64,1,128]{2,1,0:T(1,128)}), f32[64,1,128]{2,1,0:T(1,128)S(1)}, u32[]{:S(2)}, u32[]{:S(2)}) %all-to-all-start) | async-done | bytes 32800 | tf_op jit(solution)/shard_map/all_to_all | solution.py:399
  22.8 1.3 %shard_map.76 = bf16[64,16,128]{2,1,0:T(8,128)(2,1)} custom-call(f32[64,1,128]{2,1,0:T(1,128)S(1)} %all-to-all-done.index_ref, bf16[256,512]{1,0:T(8,128)(2,1)S(1)} %shard_map.75.sums_ref), custom_call_target="tpu_custom_call" | custom-call | tf_op jit(solution)/shard_map/pallas_call | solution.py:127
  24.1 7.5 %all-to-all-start.1 = ((bf16[64,16,128]{2,1,0:T(8,128)(2,1)}), bf16[64,16,128]{2,1,0:T(8,128)(2,1)S(1)}, u32[]{:S(2)}, u32[]{:S(2)}) async-start(bf16[64,16,128]{2,1,0:T(8,128)(2,1)} %shard_map.76), calls=%async_computation.1 | async-start | bytes 524288 | tf_op jit(solution)/shard_map/all_to_all | solution.py:402
  31.6 0.1 copy.10
  31.7 0.1 copy.11
  31.9 0.1 reshape.7.wave_ref
  32.0 0.0 copy-done.2
  32.0 0.0 copy-done.3
  32.0 5.6 %shard_map.74 = (bf16[4,2560,128]{2,1,0:T(8,128)(2,1)S(1)}, s32[4]{0:T(128)S(1)}) custom-call(s32[4]{0:T(128)S(1)} %copy-done.2, s32[256]{0:T(256)S(1)} %copy-done.3, f32[64,1,128]{2,1,0:T(1,128)S(1)} %all-to-all-done.index_ref), custom_call_target="tpu_custom_call" | custom-call | tf_op jit(solution)/shard_map/pallas_call | solution.py:190
  37.5 5.7 %all-to-all-done.1.got_ref = bf16[64,16,128]{2,1,0:T(8,128)(2,1)S(1)} async-done(((bf16[64,16,128]{2,1,0:T(8,128)(2,1)}), bf16[64,16,128]{2,1,0:T(8,128)(2,1)S(1)}, u32[]{:S(2)}, u32[]{:S(2)}) %all-to-all-start.1) | async-done | bytes 262176 | tf_op jit(solution)/shard_map/all_to_all | solution.py:402
  43.2 0.0 copy-done
  43.2 0.0 copy-done.1
  43.2 4.2 %shard_map.77 = bf16[8,208,128]{2,1,0:T(8,128)(2,1)S(1)} custom-call(s32[4]{0:T(128)S(1)} %get-tuple-element.7.points, bf16[64,16,128]{2,1,0:T(8,128)(2,1)S(1)} %all-to-all-done.1.got_ref, f32[1,1280]{1,0:T(1,128)S(1)} %reshape.7.wave_ref, bf16[240,128]{1,0:T(8,128)(2,1)S(1)} %copy-done, bf16[128,128]{1,0:T(8,128)(2,1)S(1)} %copy-done.1, ...), custom_call_target="tpu_custom_call" | custom-call | tf_op jit(solution)/shard_map/pallas_call | solution.py:342
  47.4 22.6 %all_to_all.15.in_ref = bf16[8,208,128]{2,1,0:T(8,128)(2,1)S(1)} all-to-all(bf16[8,208,128]{2,1,0:T(8,128)(2,1)S(1)} %shard_map.77), channel_id=1, replica_groups=mesh['wave'=64,'field'=8] {'field'}, dimensions={0} | all-to-all | bytes 851968 | tf_op jit(solution)/shard_map/all_to_all | solution.py:406
  70.0 1.0 %shard_map.78 = bf16[2,80,1289]{2,1,0:T(8,128)(2,1)} custom-call(bf16[8,208,128]{2,1,0:T(8,128)(2,1)S(1)} %all_to_all.15.in_ref), custom_call_target="tpu_custom_call" | custom-call | tf_op jit(solution)/shard_map/pallas_call | solution.py:376
  (4 shorter events, 0.0 us)
Async XLA Ops:
  1.3 21.5 %all-to-all-start = ((f32[64,1,128]{2,1,0:T(1,128)}), f32[64,1,128]{2,1,0:T(1,128)S(1)}, u32[]{:S(2)}, u32[]{:S(2)}) async-start(f32[64,1,128]{2,1,0:T(1,128)} %shard_map.73), calls=%async_computation | async-start | bytes 65536 | tf_op jit(solution)/shard_map/all_to_all | solution.py:399
  15.3 16.6 %copy-start.2 = (s32[4]{0:T(128)S(1)}, s32[4]{0:T(128)}, u32[]{:S(2)}) copy-start(s32[4]{0:T(128)} %lat_rows.1) | copy-start | bytes 52
  15.4 16.6 %copy-start.3 = (s32[256]{0:T(256)S(1)}, s32[256]{0:T(256)}, u32[]{:S(2)}) copy-start(s32[256]{0:T(256)} %npoints.1) | copy-start | bytes 3076
  15.4 27.8 %copy-start = (bf16[240,128]{1,0:T(8,128)(2,1)S(1)}, bf16[240,128]{1,0:T(8,128)(2,1)}, u32[]{:S(2)}) copy-start(bf16[240,128]{1,0:T(8,128)(2,1)} %constant.6.clone.select_ref) | copy-start | bytes 184324
  15.4 27.8 %copy-start.1 = (bf16[128,128]{1,0:T(8,128)(2,1)S(1)}, bf16[128,128]{1,0:T(8,128)(2,1)}, u32[]{:S(2)}) copy-start(bf16[128,128]{1,0:T(8,128)(2,1)} %constant.7.clone.reverse_ref) | copy-start | bytes 98308
  24.1 19.1 %all-to-all-start.1 = ((bf16[64,16,128]{2,1,0:T(8,128)(2,1)}), bf16[64,16,128]{2,1,0:T(8,128)(2,1)S(1)}, u32[]{:S(2)}, u32[]{:S(2)}) async-start(bf16[64,16,128]{2,1,0:T(8,128)(2,1)} %shard_map.76), calls=%async_computation.1 | async-start | bytes 524288 | tf_op jit(solution)/shard_map/all_to_all | solution.py:402
